TPU v7x, 512 devices: a whole 4x8x8 slice. The times are simulated.
512 devices in a mesh: plant: 8 (over x, y_hi), section: 64 (over y_lo, z, core).
Axes of the slice: x: 4, y: 8 (y_hi: 2, y_lo: 4; y = y_hi * 4 + y_lo), z: 8, core: 2. Of those that a mesh axis runs over, the one named last changes fastest.
Arguments:
- dynamics_operator: bfloat16 [4096, 512], P('plant'), parts along dimension 0
- control_gain_array: bfloat16 [4096, 256], P('plant'), parts along dimension 0
- kkt_inverse: bfloat16 [6144, 768], P('plant'), parts along dimension 0
- lin_state: float32 [4096, 16384], P(('plant', 'section')), parts along dimension 0, may hold values from -6 to 6
- lin_input: float32 [2048, 16384], P(('plant', 'section')), parts along dimension 0, may hold values from -6 to 6
- block_start: int32 [8], P('plant'), parts along dimension 0, may hold values from 0 to 63
- period: int32 [8], P('plant'), parts along dimension 0, may hold values from 8192 to 16384
Outputs:
- state_traj: float32 [4096, 16384], P('plant', 'section'), parts along dimension 0
- input_traj: float32 [2048, 16384], P('plant', 'section'), parts along dimension 0
- consensus: float32 [4096, 16384], P('plant', 'section'), parts along dimension 0
- residual_norms: float32 [16], P('plant'), parts along dimension 0
There are 8 independent parts, one for each index of `plant`. A program takes and returns all parts, laid end to end along the dimension named above; each array names one. Nothing has to cross between parts.
Inputs may be any that keep to these rules, and one draw needn't show every extreme that they name: Device d of the section axis holds the block of logical sections starting at 256 * ((d - block_start) mod the axis's size).
All inputs are finite; a program needn't handle non-finite values.
Results may differ from a plain program's by a relative error of at most 0.0045.
Values sent between devices are 32-bit elements; how exact they have to be, the bound alone decides.
No kernel may reach another device: no remote copies, remote signals or barrier semaphores. Data moves between devices by JAX's collectives and lax.ppermute only.
A program may use at most 64 MiB of HBM per device.

v0:
```python
import jax
import jax.numpy as jnp
from jax import lax
from jax.sharding import PartitionSpec as P

ITERS = 4


RHO = 1.0


def padded(cells, sides, width):
    for axis, dim in sides:
        count = lax.axis_size(axis)
        head = lax.slice_in_dim(cells, 0, width, axis=dim)
        tail = lax.slice_in_dim(cells, cells.shape[dim] - width, cells.shape[dim], axis=dim)
        cells = jnp.concatenate(
            [
                lax.ppermute(tail, axis, [(i, (i + 1) % count) for i in range(count)]),
                cells,
                lax.ppermute(head, axis, [((i + 1) % count, i) for i in range(count)]),
            ],
            axis=dim,
        )
    return cells


def copy_for_each(shard, axis):
    length = lax.axis_size(axis)
    return lax.all_to_all(
        jnp.broadcast_to(shard[None], (length, *shard.shape)), axis, 0, 0, tiled=True
    )


def over_copies(shard, axis):
    return copy_for_each(shard, axis).sum(axis=0)


def in_one(arrays, axis):
    ends = [0]
    for a in arrays:
        ends.append(ends[-1] + a.size)
    running = over_copies(jnp.concatenate([a.ravel() for a in arrays]), axis)
    return tuple((running[b:e].reshape(a.shape) for a, b, e in zip(arrays, ends, ends[1:])))


def adjoint(dynamics_operator, control_gain_array, target):
    rounded = target.astype(jnp.bfloat16)
    contract = (((0,), (0,)), ((), ()))
    upper_part = lax.dot_general(
        dynamics_operator, rounded, contract, preferred_element_type=jnp.float32
    )
    lower_part = lax.dot_general(
        control_gain_array, rounded, contract, preferred_element_type=jnp.float32
    )
    return jnp.concatenate([upper_part, lower_part], axis=0)


def estimate_condition(dynamics_operator, control_gain_array, merged_pieces, condition_lines):
    rounded = merged_pieces.astype(jnp.bfloat16)
    return jnp.dot(
        dynamics_operator, rounded[:condition_lines], preferred_element_type=jnp.float32
    ) + jnp.dot(control_gain_array, rounded[condition_lines:], preferred_element_type=jnp.float32)


def pick_column(values, selector):
    return jnp.sum(jnp.where(selector, values, 0.0), axis=1, keepdims=True)


def local(
    dynamics_operator, control_gain_array, kkt_inverse, lin_state, lin_input, block_start, period
):
    condition_lines = dynamics_operator.shape[0]
    cycle_size = lax.axis_size("section")
    block_width = lin_state.shape[1] // cycle_size
    block_index = (lax.axis_index("section") - block_start[0]) % cycle_size
    section_ids = block_index * block_width + jnp.arange(block_width, dtype=jnp.int32)
    working_segment = (section_ids < period[0])[None, :]
    is_first = (section_ids == 0)[None, :]
    is_last = (section_ids == period[0] - 1)[None, :]
    state_parts = lin_state.reshape(lin_state.shape[0], cycle_size, block_width)
    input_parts = lin_input.reshape(lin_input.shape[0], cycle_size, block_width)
    cost_state = lax.all_to_all(state_parts, "section", split_axis=1, concat_axis=0, tiled=True)
    cost_input = lax.all_to_all(input_parts, "section", split_axis=1, concat_axis=0, tiled=True)
    neg_part = -jnp.concatenate([cost_state[:, 0, :], cost_input[:, 0, :]], axis=0)
    product = jnp.dot(
        kkt_inverse, neg_part.astype(jnp.bfloat16), preferred_element_type=jnp.float32
    )
    neg_cost, product = (neg_part, product)
    zero_block = jnp.zeros((condition_lines, block_width), jnp.float32)
    input_zero = jnp.zeros((neg_cost.shape[0] - condition_lines, block_width), jnp.float32)
    consensus = zero_block
    dual_state = zero_block
    multiplier_link = zero_block
    ahead_z = zero_block
    merged_pieces = jnp.zeros_like(neg_cost)
    primal_part = jnp.float32(0.0)
    dual_part = jnp.float32(0.0)
    for iteration in range(ITERS):
        if iteration > 0:
            right_side = (
                neg_cost
                + RHO * jnp.concatenate([consensus - dual_state, input_zero], axis=0)
                + RHO * adjoint(dynamics_operator, control_gain_array, ahead_z - multiplier_link)
            )
            product = jnp.dot(
                kkt_inverse, right_side.astype(jnp.bfloat16), preferred_element_type=jnp.float32
            )
        merged_pieces = jnp.where(working_segment, product, 0.0)
        expected_condition = estimate_condition(
            dynamics_operator, control_gain_array, merged_pieces, condition_lines
        )
        own_sum = merged_pieces[:condition_lines] + dual_state
        passed_quantity = expected_condition + multiplier_link
        stacked = jnp.concatenate([passed_quantity, own_sum], axis=0)
        edges = jnp.concatenate([stacked[:, :1], stacked[:, -1:]], axis=1)
        rim_cols = padded(edges, (("section", 1),), 1)
        closing_carried, closing_own = in_one(
            (pick_column(passed_quantity, is_last), pick_column(own_sum, is_first)), "section"
        )
        previous = jnp.concatenate(
            [rim_cols[:condition_lines, 0:1], passed_quantity[:, :-1]], axis=1
        )
        previous = jnp.where(is_first, closing_carried, previous)
        newest_agreement = jnp.where(working_segment, 0.5 * (own_sum + previous), 0.0)
        ahead_tail = 0.5 * (rim_cols[condition_lines:, -1:] + passed_quantity[:, -1:])
        onward_refreshed = jnp.concatenate([newest_agreement[:, 1:], ahead_tail], axis=1)
        onward_refreshed = jnp.where(
            is_last, 0.5 * (closing_own + closing_carried), onward_refreshed
        )
        change_z = newest_agreement - consensus
        dual_state = jnp.where(
            working_segment, dual_state + merged_pieces[:condition_lines] - newest_agreement, 0.0
        )
        multiplier_link = jnp.where(
            working_segment, multiplier_link + expected_condition - onward_refreshed, 0.0
        )
        if iteration == ITERS - 1:
            primal_part = jnp.sum(
                jnp.where(
                    working_segment,
                    (merged_pieces[:condition_lines] - newest_agreement) ** 2
                    + (expected_condition - onward_refreshed) ** 2,
                    0.0,
                )
            )
            dual_part = RHO * RHO * jnp.sum(change_z * change_z)
        consensus = newest_agreement
        ahead_z = onward_refreshed
    primal_total, dual_total = in_one((primal_part, dual_part), "section")
    residual_norms = jnp.stack([jnp.sqrt(primal_total), jnp.sqrt(dual_total)])
    return (
        merged_pieces[:condition_lines],
        merged_pieces[condition_lines:],
        consensus,
        residual_norms,
    )


def solution(mesh):
    return jax.shard_map(
        local,
        mesh=mesh,
        in_specs=(
            P("plant", None),
            P("plant", None),
            P("plant", None),
            P(("plant", "section"), None),
            P(("plant", "section"), None),
            P("plant"),
            P("plant"),
        ),
        out_specs=(P("plant", "section"), P("plant", "section"), P("plant", "section"), P("plant")),
        check_vma=False,
    )
```

profile of v0, /device:TPU:1, one launch (start us, length us, event | category | flops | bytes accessed | tf_op | source)
XLA Modules:
  0.0 179.3 jit_solution(17230519202010785771)
XLA Ops:
  0.6 27.2 %all_to_all.60 = f32[4,64,256]{2,0,1:T(4,128)S(1)} all-to-all(f32[4,64,256]{2,0,1:T(4,128)} %bitcast.86), channel_id=1, replica_groups=mesh['plant'=8,'section'=64] {'section'}, dimensions={1} | all-to-all | bytes 524288 | tf_op jit(solution)/shard_map/all_to_all | solution.py:84
  27.8 6.0 %all-to-all-start = ((f32[8,64,256]{2,0,1:T(8,128)}), f32[8,64,256]{2,0,1:T(8,128)S(1)}, u32[]{:S(2)}, u32[]{:S(2)}) async-start(f32[8,64,256]{2,0,1:T(8,128)} %bitcast.85), calls=%async_computation | async-start | bytes 1048576 | tf_op jit(solution)/shard_map/all_to_all | solution.py:83
  35.4 15.6 %all-to-all-done = f32[8,64,256]{2,0,1:T(8,128)S(1)} async-done(((f32[8,64,256]{2,0,1:T(8,128)}), f32[8,64,256]{2,0,1:T(8,128)S(1)}, u32[]{:S(2)}, u32[]{:S(2)}) %all-to-all-start) | async-done | bytes 524320 | tf_op jit(solution)/shard_map/all_to_all | solution.py:83
  54.6 6.1 %all-to-all-start.2 = ((f32[64,1,1024]{2,1,0:T(1,128)}), f32[64,1,1024]{2,1,0:T(1,128)S(1)}, u32[]{:S(2)}, u32[]{:S(2)}) async-start(f32[64,1,1024]{2,1,0:T(1,128)} %broadcast_in_dim.222), calls=%async_computation.2 | async-start | bytes 524288 | tf_op jit(solution)/shard_map/all_to_all | solution.py:30
  61.4 3.5 %collective-permute-start = (f32[1024,1]{0,1:T(1,128)S(1)}, f32[1024,1]{0,1:T(1,128)S(1)}, u32[]{:S(2)}, u32[]{:S(2)}) collective-permute-start(f32[1024,1]{0,1:T(1,128)S(1)} %get-tuple-element.42), channel_id=1, source_target_pairs={{0,1},{1,2},{2,3},{3,4},{4,5},{5,6},{6,7},{7,8},{8,9},{9,10},{10,1... | collective-permute-start | bytes 12296 | tf_op jit(solution)/shard_map/ppermute | solution.py:19
  65.0 1.9 %collective-permute-start.1 = (f32[1024,1]{0,1:T(1,128)S(1)}, f32[1024,1]{0,1:T(1,128)S(1)}, u32[]{:S(2)}, u32[]{:S(2)}) collective-permute-start(f32[1024,1]{0,1:T(1,128)S(1)} %get-tuple-element.43), channel_id=1, source_target_pairs={{1,0},{2,1},{3,2},{4,3},{5,4},{6,5},{7,6},{8,7},{9,8},{10,9},{11,1... | collective-permute-start | bytes 12296 | tf_op jit(solution)/shard_map/ppermute | solution.py:21
  67.5 2.7 %collective-permute-done.1 = f32[1024,1]{0,1:T(1,128)S(1)} collective-permute-done((f32[1024,1]{0,1:T(1,128)S(1)}, f32[1024,1]{0,1:T(1,128)S(1)}, u32[]{:S(2)}, u32[]{:S(2)}) %collective-permute-start.1) | collective-permute-done | bytes 4128 | tf_op jit(solution)/shard_map/ppermute | solution.py:21
  70.2 2.1 %all-to-all-done.2 = f32[64,1,1024]{2,1,0:T(1,128)S(1)} async-done(((f32[64,1,1024]{2,1,0:T(1,128)}), f32[64,1,1024]{2,1,0:T(1,128)S(1)}, u32[]{:S(2)}, u32[]{:S(2)}) %all-to-all-start.2) | async-done | bytes 262176 | tf_op jit(solution)/shard_map/all_to_all | solution.py:30
  73.9 1.3 fusion.30
  79.6 8.4 %all-to-all-start.3 = ((f32[64,1,1024]{2,1,0:T(1,128)}), f32[64,1,1024]{2,1,0:T(1,128)}, u32[]{:S(2)}, u32[]{:S(2)}) async-start(f32[64,1,1024]{2,1,0:T(1,128)} %broadcast_in_dim.225), calls=%async_computation.3 | async-start | bytes 524288 | tf_op jit(solution)/shard_map/all_to_all | solution.py:30
  88.7 3.5 %collective-permute-start.2 = (f32[1024,1]{0,1:T(1,128)S(1)}, f32[1024,1]{0,1:T(1,128)S(1)}, u32[]{:S(2)}, u32[]{:S(2)}) collective-permute-start(f32[1024,1]{0,1:T(1,128)S(1)} %get-tuple-element.40), channel_id=1, source_target_pairs={{0,1},{1,2},{2,3},{3,4},{4,5},{5,6},{6,7},{7,8},{8,9},{9,10},{10,1... | collective-permute-start | bytes 12296 | tf_op jit(solution)/shard_map/ppermute | solution.py:19
  92.2 1.9 %collective-permute-start.3 = (f32[1024,1]{0,1:T(1,128)S(1)}, f32[1024,1]{0,1:T(1,128)S(1)}, u32[]{:S(2)}, u32[]{:S(2)}) collective-permute-start(f32[1024,1]{0,1:T(1,128)S(1)} %get-tuple-element.41), channel_id=1, source_target_pairs={{1,0},{2,1},{3,2},{4,3},{5,4},{6,5},{7,6},{8,7},{9,8},{10,9},{11,1... | collective-permute-start | bytes 12296 | tf_op jit(solution)/shard_map/ppermute | solution.py:21
  94.7 3.0 %collective-permute-done.3 = f32[1024,1]{0,1:T(1,128)S(1)} collective-permute-done((f32[1024,1]{0,1:T(1,128)S(1)}, f32[1024,1]{0,1:T(1,128)S(1)}, u32[]{:S(2)}, u32[]{:S(2)}) %collective-permute-start.3) | collective-permute-done | bytes 4128 | tf_op jit(solution)/shard_map/ppermute | solution.py:21
  97.7 1.8 %all-to-all-done.3 = f32[64,1,1024]{2,1,0:T(1,128)} async-done(((f32[64,1,1024]{2,1,0:T(1,128)}), f32[64,1,1024]{2,1,0:T(1,128)}, u32[]{:S(2)}, u32[]{:S(2)}) %all-to-all-start.3) | async-done | bytes 262176 | tf_op jit(solution)/shard_map/all_to_all | solution.py:30
  99.6 1.7 reduce_sum.140
  107.2 8.4 %all-to-all-start.4 = ((f32[64,1,1024]{2,1,0:T(1,128)}), f32[64,1,1024]{2,1,0:T(1,128)}, u32[]{:S(2)}, u32[]{:S(2)}) async-start(f32[64,1,1024]{2,1,0:T(1,128)} %broadcast_in_dim.228), calls=%async_computation.4 | async-start | bytes 524288 | tf_op jit(solution)/shard_map/all_to_all | solution.py:30
  116.4 3.5 %collective-permute-start.4 = (f32[1024,1]{0,1:T(1,128)S(1)}, f32[1024,1]{0,1:T(1,128)S(1)}, u32[]{:S(2)}, u32[]{:S(2)}) collective-permute-start(f32[1024,1]{0,1:T(1,128)S(1)} %get-tuple-element.38), channel_id=1, source_target_pairs={{0,1},{1,2},{2,3},{3,4},{4,5},{5,6},{6,7},{7,8},{8,9},{9,10},{10,1... | collective-permute-start | bytes 12296 | tf_op jit(solution)/shard_map/ppermute | solution.py:19
  119.9 2.1 %collective-permute-start.5 = (f32[1024,1]{0,1:T(1,128)S(1)}, f32[1024,1]{0,1:T(1,128)S(1)}, u32[]{:S(2)}, u32[]{:S(2)}) collective-permute-start(f32[1024,1]{0,1:T(1,128)S(1)} %get-tuple-element.39), channel_id=1, source_target_pairs={{1,0},{2,1},{3,2},{4,3},{5,4},{6,5},{7,6},{8,7},{9,8},{10,9},{11,1... | collective-permute-start | bytes 12296 | tf_op jit(solution)/shard_map/ppermute | solution.py:21
  122.6 2.8 %collective-permute-done.5 = f32[1024,1]{0,1:T(1,128)S(1)} collective-permute-done((f32[1024,1]{0,1:T(1,128)S(1)}, f32[1024,1]{0,1:T(1,128)S(1)}, u32[]{:S(2)}, u32[]{:S(2)}) %collective-permute-start.5) | collective-permute-done | bytes 4128 | tf_op jit(solution)/shard_map/ppermute | solution.py:21
  125.4 1.8 %all-to-all-done.4 = f32[64,1,1024]{2,1,0:T(1,128)} async-done(((f32[64,1,1024]{2,1,0:T(1,128)}), f32[64,1,1024]{2,1,0:T(1,128)}, u32[]{:S(2)}, u32[]{:S(2)}) %all-to-all-start.4) | async-done | bytes 262176 | tf_op jit(solution)/shard_map/all_to_all | solution.py:30
  127.2 1.7 reduce_sum.143
  132.8 1.2 select_reduce_fusion.1
  134.0 1.0 broadcast_in_dim.231
  135.0 8.2 %all-to-all-start.5 = ((f32[64,1,1024]{2,1,0:T(1,128)}), f32[64,1,1024]{2,1,0:T(1,128)S(1)}, u32[]{:S(2)}, u32[]{:S(2)}) async-start(f32[64,1,1024]{2,1,0:T(1,128)} %broadcast_in_dim.231), calls=%async_computation.5 | async-start | bytes 524288 | tf_op jit(solution)/shard_map/all_to_all | solution.py:30
  143.2 3.5 %collective-permute-start.6 = (f32[1024,1]{0,1:T(1,128)S(1)}, f32[1024,1]{0,1:T(1,128)S(1)}, u32[]{:S(2)}, u32[]{:S(2)}) collective-permute-start(f32[1024,1]{0,1:T(1,128)S(1)} %get-tuple-element.37), channel_id=1, source_target_pairs={{0,1},{1,2},{2,3},{3,4},{4,5},{5,6},{6,7},{7,8},{8,9},{9,10},{10,1... | collective-permute-start | bytes 12296 | tf_op jit(solution)/shard_map/ppermute | solution.py:19
  146.7 1.9 %collective-permute-start.7 = (f32[1024,1]{0,1:T(1,128)S(1)}, f32[1024,1]{0,1:T(1,128)S(1)}, u32[]{:S(2)}, u32[]{:S(2)}) collective-permute-start(f32[1024,1]{0,1:T(1,128)S(1)} %get-tuple-element.36), channel_id=1, source_target_pairs={{1,0},{2,1},{3,2},{4,3},{5,4},{6,5},{7,6},{8,7},{9,8},{10,9},{11,1... | collective-permute-start | bytes 12296 | tf_op jit(solution)/shard_map/ppermute | solution.py:21
  148.7 3.3 %collective-permute-done.7 = f32[1024,1]{0,1:T(1,128)S(1)} collective-permute-done((f32[1024,1]{0,1:T(1,128)S(1)}, f32[1024,1]{0,1:T(1,128)S(1)}, u32[]{:S(2)}, u32[]{:S(2)}) %collective-permute-start.7) | collective-permute-done | bytes 4128 | tf_op jit(solution)/shard_map/ppermute | solution.py:21
  152.0 2.8 %all-to-all-done.5 = f32[64,1,1024]{2,1,0:T(1,128)S(1)} async-done(((f32[64,1,1024]{2,1,0:T(1,128)}), f32[64,1,1024]{2,1,0:T(1,128)S(1)}, u32[]{:S(2)}, u32[]{:S(2)}) %all-to-all-start.5) | async-done | bytes 262176 | tf_op jit(solution)/shard_map/all_to_all | solution.py:30
  155.1 1.5 fusion.24
  157.8 1.4 pad_maximum_fusion.12
  159.8 7.5 %all-to-all-start.6 = ((f32[64,1,2]{2,1,0:T(1,128)}), f32[64,1,2]{2,1,0:T(1,128)S(1)}, u32[]{:S(2)}, u32[]{:S(2)}) async-start(f32[64,1,2]{2,1,0:T(1,128)} %broadcast_in_dim.234), calls=%async_computation.6 | async-start | bytes 65536 | tf_op jit(solution)/shard_map/all_to_all | solution.py:30
  170.1 6.7 %all-to-all-done.6 = f32[64,1,2]{2,1,0:T(1,128)S(1)} async-done(((f32[64,1,2]{2,1,0:T(1,128)}), f32[64,1,2]{2,1,0:T(1,128)S(1)}, u32[]{:S(2)}, u32[]{:S(2)}) %all-to-all-start.6) | async-done | bytes 544 | tf_op jit(solution)/shard_map/all_to_all | solution.py:30
  (106 shorter events, 29.4 us)
Async XLA Ops:
  0.6 50.6 %copy-start = (bf16[768,768]{1,0:T(8,128)(2,1)S(1)}, bf16[768,768]{1,0:T(8,128)(2,1)}, u32[]{:S(2)}) copy-start(bf16[768,768]{1,0:T(8,128)(2,1)} %param.9) | copy-start | bytes 3538948
  27.8 23.2 %all-to-all-start = ((f32[8,64,256]{2,0,1:T(8,128)}), f32[8,64,256]{2,0,1:T(8,128)S(1)}, u32[]{:S(2)}, u32[]{:S(2)}) async-start(f32[8,64,256]{2,0,1:T(8,128)} %bitcast.85), calls=%async_computation | async-start | bytes 1048576 | tf_op jit(solution)/shard_map/all_to_all | solution.py:83
  35.4 40.5 %copy-start.9 = (f32[256,256]{0,1:T(8,128)}, f32[256,256]{0,1:T(8,128)S(1)}, u32[]{:S(2)}) copy-start(f32[256,256]{0,1:T(8,128)S(1)} %copy.33) | copy-start | bytes 786436
  51.2 1.0 copy-start.1
  51.7 1.7 copy-start.7
  52.2 1.2 copy-start.2
  54.6 17.7 %all-to-all-start.2 = ((f32[64,1,1024]{2,1,0:T(1,128)}), f32[64,1,1024]{2,1,0:T(1,128)S(1)}, u32[]{:S(2)}, u32[]{:S(2)}) async-start(f32[64,1,1024]{2,1,0:T(1,128)} %broadcast_in_dim.222), calls=%async_computation.2 | async-start | bytes 524288 | tf_op jit(solution)/shard_map/all_to_all | solution.py:30
  61.4 5.5 %collective-permute-start = (f32[1024,1]{0,1:T(1,128)S(1)}, f32[1024,1]{0,1:T(1,128)S(1)}, u32[]{:S(2)}, u32[]{:S(2)}) collective-permute-start(f32[1024,1]{0,1:T(1,128)S(1)} %get-tuple-element.42), channel_id=1, source_target_pairs={{0,1},{1,2},{2,3},{3,4},{4,5},{5,6},{6,7},{7,8},{8,9},{9,10},{10,1... | collective-permute-start | bytes 12296 | tf_op jit(solution)/shard_map/ppermute | solution.py:19
  65.0 5.2 %collective-permute-start.1 = (f32[1024,1]{0,1:T(1,128)S(1)}, f32[1024,1]{0,1:T(1,128)S(1)}, u32[]{:S(2)}, u32[]{:S(2)}) collective-permute-start(f32[1024,1]{0,1:T(1,128)S(1)} %get-tuple-element.43), channel_id=1, source_target_pairs={{1,0},{2,1},{3,2},{4,3},{5,4},{6,5},{7,6},{8,7},{9,8},{10,9},{11,1... | collective-permute-start | bytes 12296 | tf_op jit(solution)/shard_map/ppermute | solution.py:21
  75.9 1.1 copy-start.8
  78.7 23.4 %copy-start.4 = (f32[512,256]{0,1:T(8,128)S(1)}, f32[512,256]{0,1:T(8,128)}, u32[]{:S(2)}) copy-start(f32[512,256]{0,1:T(8,128)} %get-tuple-element.33) | copy-start | bytes 1572868
  79.6 20.0 %all-to-all-start.3 = ((f32[64,1,1024]{2,1,0:T(1,128)}), f32[64,1,1024]{2,1,0:T(1,128)}, u32[]{:S(2)}, u32[]{:S(2)}) async-start(f32[64,1,1024]{2,1,0:T(1,128)} %broadcast_in_dim.225), calls=%async_computation.3 | async-start | bytes 524288 | tf_op jit(solution)/shard_map/all_to_all | solution.py:30
  88.7 5.5 %collective-permute-start.2 = (f32[1024,1]{0,1:T(1,128)S(1)}, f32[1024,1]{0,1:T(1,128)S(1)}, u32[]{:S(2)}, u32[]{:S(2)}) collective-permute-start(f32[1024,1]{0,1:T(1,128)S(1)} %get-tuple-element.40), channel_id=1, source_target_pairs={{0,1},{1,2},{2,3},{3,4},{4,5},{5,6},{6,7},{7,8},{8,9},{9,10},{10,1... | collective-permute-start | bytes 12296 | tf_op jit(solution)/shard_map/ppermute | solution.py:19
  92.2 5.5 %collective-permute-start.3 = (f32[1024,1]{0,1:T(1,128)S(1)}, f32[1024,1]{0,1:T(1,128)S(1)}, u32[]{:S(2)}, u32[]{:S(2)}) collective-permute-start(f32[1024,1]{0,1:T(1,128)S(1)} %get-tuple-element.41), channel_id=1, source_target_pairs={{1,0},{2,1},{3,2},{4,3},{5,4},{6,5},{7,6},{8,7},{9,8},{10,9},{11,1... | collective-permute-start | bytes 12296 | tf_op jit(solution)/shard_map/ppermute | solution.py:21
  103.2 1.0 copy-start.10
  106.4 23.4 %copy-start.3 = (f32[512,256]{0,1:T(8,128)S(1)}, f32[512,256]{0,1:T(8,128)}, u32[]{:S(2)}) copy-start(f32[512,256]{0,1:T(8,128)} %get-tuple-element.29) | copy-start | bytes 1572868
  107.2 20.0 %all-to-all-start.4 = ((f32[64,1,1024]{2,1,0:T(1,128)}), f32[64,1,1024]{2,1,0:T(1,128)}, u32[]{:S(2)}, u32[]{:S(2)}) async-start(f32[64,1,1024]{2,1,0:T(1,128)} %broadcast_in_dim.228), calls=%async_computation.4 | async-start | bytes 524288 | tf_op jit(solution)/shard_map/all_to_all | solution.py:30
  116.4 5.6 %collective-permute-start.4 = (f32[1024,1]{0,1:T(1,128)S(1)}, f32[1024,1]{0,1:T(1,128)S(1)}, u32[]{:S(2)}, u32[]{:S(2)}) collective-permute-start(f32[1024,1]{0,1:T(1,128)S(1)} %get-tuple-element.38), channel_id=1, source_target_pairs={{0,1},{1,2},{2,3},{3,4},{4,5},{5,6},{6,7},{7,8},{8,9},{9,10},{10,1... | collective-permute-start | bytes 12296 | tf_op jit(solution)/shard_map/ppermute | solution.py:19
  119.9 5.5 %collective-permute-start.5 = (f32[1024,1]{0,1:T(1,128)S(1)}, f32[1024,1]{0,1:T(1,128)S(1)}, u32[]{:S(2)}, u32[]{:S(2)}) collective-permute-start(f32[1024,1]{0,1:T(1,128)S(1)} %get-tuple-element.39), channel_id=1, source_target_pairs={{1,0},{2,1},{3,2},{4,3},{5,4},{6,5},{7,6},{8,7},{9,8},{10,9},{11,1... | collective-permute-start | bytes 12296 | tf_op jit(solution)/shard_map/ppermute | solution.py:21
  130.6 2.1 %copy-start.5 = (f32[512,256]{0,1:T(8,128)}, f32[512,256]{0,1:T(8,128)S(1)}, u32[]{:S(2)}) copy-start(f32[512,256]{0,1:T(8,128)S(1)} %get-tuple-element.27) | copy-start | bytes 1572868
  130.9 1.0 copy-start.11
  132.4 1.5 copy-start.12
  134.0 21.0 %copy-start.14 = (f32[512,256]{0,1:T(8,128)}, f32[512,256]{0,1:T(8,128)S(1)}, u32[]{:S(2)}) copy-start(f32[512,256]{0,1:T(8,128)S(1)} %get-tuple-element.23) | copy-start | bytes 1572868
  134.0 21.1 %copy-start.15 = (f32[512,256]{0,1:T(8,128)}, f32[512,256]{0,1:T(8,128)S(1)}, u32[]{:S(2)}) copy-start(f32[512,256]{0,1:T(8,128)S(1)} %get-tuple-element.58) | copy-start | bytes 1572868
  135.0 19.8 %all-to-all-start.5 = ((f32[64,1,1024]{2,1,0:T(1,128)}), f32[64,1,1024]{2,1,0:T(1,128)S(1)}, u32[]{:S(2)}, u32[]{:S(2)}) async-start(f32[64,1,1024]{2,1,0:T(1,128)} %broadcast_in_dim.231), calls=%async_computation.5 | async-start | bytes 524288 | tf_op jit(solution)/shard_map/all_to_all | solution.py:30
  143.2 5.5 %collective-permute-start.6 = (f32[1024,1]{0,1:T(1,128)S(1)}, f32[1024,1]{0,1:T(1,128)S(1)}, u32[]{:S(2)}, u32[]{:S(2)}) collective-permute-start(f32[1024,1]{0,1:T(1,128)S(1)} %get-tuple-element.37), channel_id=1, source_target_pairs={{0,1},{1,2},{2,3},{3,4},{4,5},{5,6},{6,7},{7,8},{8,9},{9,10},{10,1... | collective-permute-start | bytes 12296 | tf_op jit(solution)/shard_map/ppermute | solution.py:19
  146.7 5.2 %collective-permute-start.7 = (f32[1024,1]{0,1:T(1,128)S(1)}, f32[1024,1]{0,1:T(1,128)S(1)}, u32[]{:S(2)}, u32[]{:S(2)}) collective-permute-start(f32[1024,1]{0,1:T(1,128)S(1)} %get-tuple-element.36), channel_id=1, source_target_pairs={{1,0},{2,1},{3,2},{4,3},{5,4},{6,5},{7,6},{8,7},{9,8},{10,9},{11,1... | collective-permute-start | bytes 12296 | tf_op jit(solution)/shard_map/ppermute | solution.py:21
  155.0 1.6 copy-start.6
  155.0 1.6 copy-start.13
  155.0 1.7 copy-start.16
  159.8 17.1 %all-to-all-start.6 = ((f32[64,1,2]{2,1,0:T(1,128)}), f32[64,1,2]{2,1,0:T(1,128)S(1)}, u32[]{:S(2)}, u32[]{:S(2)}) async-start(f32[64,1,2]{2,1,0:T(1,128)} %broadcast_in_dim.234), calls=%async_computation.6 | async-start | bytes 65536 | tf_op jit(solution)/shard_map/all_to_all | solution.py:30
where the time goes:
time: 181 us; the launch traced here: 179 us
  starting transfers between devices  66.5 us (37%)
  waiting for transfers between devices  42.7 us (24%)
  blocking collectives  27.2 us (15%)
  other arithmetic  20 us (11%)
  local copies, waits for them, and re-layouts  12 us (7%)
  matrix products  7.13 us (4%)
  between operations  3.84 us (2%)
    all_to_all x5, starting transfers between devices, copy_for_each(): lax.all_to_all(jnp.broadcast_to(shard[None], (length, *shard.shape)), axi...  38.5 us
    all_to_all x1, blocking collectives, local(): lax.all_to_all(input_parts, 'section', split_axis=1, concat_axis=0, tiled...  27.2 us
    all_to_all x1, waiting for transfers between devices, local(): lax.all_to_all(state_parts, 'section', split_axis=1, concat_axis=0, tiled...  15.6 us
    all_to_all x5, waiting for transfers between devices, copy_for_each(): lax.all_to_all(jnp.broadcast_to(shard[None], (length, *shard.shape)), axi...  15.4 us
    ppermute x4, starting transfers between devices, padded(): lax.ppermute(tail, axis, [(i, (i + 1) % count) for i in range(count)])  14.1 us
    ppermute x4, waiting for transfers between devices, padded(): lax.ppermute(head, axis, [((i + 1) % count, i) for i in range(count)])  11.8 us
    ppermute x4, starting transfers between devices, padded(): lax.ppermute(head, axis, [((i + 1) % count, i) for i in range(count)])  7.86 us
    all_to_all x1, starting transfers between devices, local(): lax.all_to_all(state_parts, 'section', split_axis=1, concat_axis=0, tiled...  6 us
  transfers between devices with their start and end apart: 14, of which 10 were waited for; matrix products, arithmetic and copies ran while one was open for 4% of the time, Pallas kernels for 0%

commit v1 on v0

v1 whole, which is shorter than its diff:
```python
import jax
import jax.numpy as jnp
from jax import lax
from jax.experimental import pallas as pl
from jax.experimental.pallas import tpu as pltpu
from jax.sharding import PartitionSpec as P

ITERS = 4
RHO = 1.0
LANES = 128
HALO = 4


def pack(block_start, period, state, inputs, parts):
    rows_state, total = state.shape
    rows_input = inputs.shape[0]
    width = total // parts
    per = 2 * rows_state + 2 * rows_input + 1
    assert width == 2 * LANES and rows_state == 8 and rows_input == 4

    def body(bs_ref, pe_ref, st_ref, in_ref, out_ref, flat_ref, halo_ref):
        bs = bs_ref[0]
        pe = pe_ref[0]
        lane = lax.broadcasted_iota(jnp.int32, (16, LANES), 1)

        def tile(position):
            at = pl.ds(pl.multiple_of(position, LANES), LANES)
            return jnp.concatenate(
                [st_ref[:, at], in_ref[:, at], jnp.zeros((4, LANES), jnp.float32)], axis=0
            )

        first = tile(bs * width)
        onward = pltpu.roll(first, lax.rem(pe, LANES), 1)
        edges = []
        for q in range(4):
            collected = jnp.zeros((16, LANES), jnp.float32)
            for e in range(16):
                d = 16 * q + e
                ends = []
                for half in range(2):
                    at = (2 * d + half) * LANES
                    section = lax.rem(at - bs * width + total, total)
                    beyond = lane + (section - pe)
                    wraps = (beyond >= 0) & (beyond < HALO)
                    cut = jnp.where(wraps, onward, tile(at))
                    out_ref[per * d + 8 * half : per * d + 8 * half + 8, :] = cut[:8]
                    out_ref[per * d + 16 + 4 * half : per * d + 20 + 4 * half, :] = cut[8:12]
                    ends.append(cut)
                both = jnp.where(lane < HALO, ends[0], ends[1])
                shift = (8 * e + HALO) % LANES
                both = pltpu.roll(both, shift, 1) if shift else both
                collected = jnp.where((lane >> 3) == e, both, collected)
            edges.append(collected)
        before = lax.rem(bs + parts - 1, parts)
        late = lax.rem(pe - HALO, LANES)
        tail_at = lax.rem(pe - HALO - late + bs * width, total)
        tail_next = lax.rem(tail_at + LANES, total)
        tail = jnp.where(lane >= late, tile(tail_at), tile(tail_next))
        tail = pltpu.roll(tail, lax.rem(8 * lax.rem(before, 16) - late + LANES, LANES), 1)
        skip = total - pe
        skip = jnp.where(skip < HALO, skip, 0)
        head = pltpu.roll(first, lax.rem(8 * lax.rem(bs, 16) + HALO - skip + LANES, LANES), 1)
        for q in range(4):
            block = 16 * q + (lane >> 3)
            slot = lane & 7
            value = jnp.where((block == before) & (slot < HALO), tail, edges[q])
            value = jnp.where((block == bs) & (slot >= HALO), head, value)
            flat_ref[LANES * q : LANES * q + LANES, 0:16] = value.T
        for h in range(8):
            halo_ref[:, 16 * h : 16 * h + 16] = flat_ref[pl.ds(h, parts, stride=8), 0:16]
        flat = halo_ref[...]
        lane = lax.broadcasted_iota(jnp.int32, (parts, LANES), 1)
        out_ref[pl.ds(per - 1, parts, stride=per), :] = jnp.where(
            lane < 64, pltpu.roll(flat, 1, 0), pltpu.roll(flat, parts - 1, 0)
        )

    smem = pl.BlockSpec(memory_space=pltpu.SMEM)
    vmem = pl.BlockSpec(memory_space=pltpu.VMEM)
    return pl.pallas_call(
        body,
        name="pack",
        out_shape=jax.ShapeDtypeStruct((parts * per, LANES), jnp.float32),
        in_specs=[smem, smem, vmem, vmem],
        out_specs=vmem,
        scratch_shapes=[
            pltpu.VMEM((4 * LANES, LANES), jnp.float32),
            pltpu.VMEM((parts, LANES), jnp.float32),
        ],
        compiler_params=pltpu.CompilerParams(vmem_limit_bytes=32 << 20),
    )(block_start, period, state, inputs)


def iterate(block_start, period, received, dynamics, gain, inverse, parts):
    states = dynamics.shape[0]
    controls = gain.shape[1]
    both = states + controls
    width = 2 * LANES
    rows = width + 2 * HALO
    per = received.shape[0] // parts
    nt = (((1,), (1,)), ((), ()))
    nn = (((1,), (0,)), ((), ()))
    tn = (((0,), (0,)), ((), ()))

    def body(bs_ref, pe_ref, got_ref, a_ref, b_ref, k_ref, x_ref, u_ref, z_ref, sums_ref,
             neg_ref, w_ref, zs_ref, ys_ref, vs_ref, gn_ref):
        sub = lax.broadcasted_iota(jnp.int32, (8, LANES), 0)
        for g in range(states // LANES):
            for j in range(2):
                block = jnp.concatenate(
                    [got_ref[per * s + 8 * j : per * s + 8 * j + 8, :] for s in range(16 * g, 16 * g + 16)], axis=0
                )
                neg_ref[LANES * j : LANES * j + LANES, LANES * g : LANES * g + LANES] = -block.T
        for g in range(controls // LANES):
            halves = ([], [])
            for s in range(32 * g, 32 * g + 32, 2):
                one = got_ref[per * s + 16 : per * s + 24, :]
                two = got_ref[per * (s + 1) + 16 : per * (s + 1) + 24, :]
                halves[0].append(jnp.where(sub < 4, one, pltpu.roll(two, 4, 0)))
                halves[1].append(jnp.where(sub < 4, pltpu.roll(one, 4, 0), two))
            for j in range(2):
                at = states + LANES * g
                neg_ref[LANES * j : LANES * j + LANES, at : at + LANES] = -jnp.concatenate(halves[j], axis=0).T
        edge = got_ref[pl.ds(per - 1, parts, stride=per), :]
        high = edge.astype(jnp.bfloat16)
        rest = edge - high.astype(jnp.float32)
        middle = rest.astype(jnp.bfloat16)
        low = (rest - middle.astype(jnp.float32)).astype(jnp.bfloat16)
        cut = jnp.concatenate([high, middle, low], axis=0)
        src = lax.broadcasted_iota(jnp.int32, (3 * parts, both), 0) & (parts - 1)
        col = lax.broadcasted_iota(jnp.int32, (3 * parts, both), 1)
        owner = jnp.where(col < states, col >> 3, (col - states) >> 2)
        spread = jnp.where(owner == src, 1.0, 0.0).astype(jnp.bfloat16)
        wide = lax.dot_general(cut, spread, tn, preferred_element_type=jnp.float32)
        slot = lax.broadcasted_iota(jnp.int32, (LANES, both), 0) & 15
        col = lax.broadcasted_iota(jnp.int32, (LANES, both), 1)
        place = jnp.where(col < states, col & 7, 8 + (col & 3))
        wide = jnp.where(slot == place, wide, 0.0).reshape(8, 16, both).sum(axis=1)
        neg_ref[width : width + 8, :] = -pltpu.roll(wide, HALO, 0)

        for it in range(ITERS):
            last = it == ITERS - 1
            if it == 0:
                rhs = neg_ref[...].astype(jnp.bfloat16)
            else:
                g = gn_ref[...]
                t_s = lax.dot_general(g, a_ref[...], nn, preferred_element_type=jnp.float32)
                t_u = lax.dot_general(g, b_ref[...], nn, preferred_element_type=jnp.float32)
                rhs = jnp.concatenate(
                    [
                        (neg_ref[:, :states] + RHO * (zs_ref[...] - ys_ref[...]) + RHO * t_s).astype(jnp.bfloat16),
                        (neg_ref[:, states:] + RHO * t_u).astype(jnp.bfloat16),
                    ],
                    axis=1,
                )
            w = lax.dot_general(rhs, k_ref[...], nt, preferred_element_type=jnp.float32)
            x = w[:, :states]
            wb = w.astype(jnp.bfloat16)
            pred = lax.dot_general(wb[:, :states], a_ref[...], nt, preferred_element_type=jnp.float32)
            pred = pred + lax.dot_general(wb[:, states:], b_ref[...], nt, preferred_element_type=jnp.float32)
            if it == 0:
                a, p = x, pred
            else:
                a, p = x + ys_ref[...], pred + vs_ref[...]
            znew = 0.5 * (a + pltpu.roll(p, 1, 0))
            znn = pltpu.roll(znew, rows - 1, 0)
            if not last:
                ys_ref[...] = a - znew
                v = p - znn
                vs_ref[...] = v
                gn_ref[...] = (znn - v).astype(jnp.bfloat16)
                zs_ref[...] = znew
            else:
                idx = lax.rem(lax.axis_index("section") - bs_ref[0] + parts, parts)
                count = pe_ref[0] - idx * width
                here = lax.broadcasted_iota(jnp.int32, (width, states), 0) < count
                gap = (x - znew)[:width]
                miss = (pred - znn)[:width]
                step = znew[:width] - zs_ref[:width, :]
                primal = jnp.sum(jnp.where(here, gap * gap + miss * miss, 0.0))
                dual = RHO * RHO * jnp.sum(jnp.where(here, step * step, 0.0))
                lane = lax.broadcasted_iota(jnp.int32, (parts, LANES), 1)
                sums_ref[...] = jnp.where(lane == 0, primal, jnp.where(lane == 1, dual, 0.0))
                keep = lax.broadcasted_iota(jnp.int32, (states, width), 1) < count
                x_ref[...] = jnp.where(keep, x[:width].T, 0.0)
                z_ref[...] = jnp.where(keep, znew[:width].T, 0.0)
                u_ref[...] = jnp.where(keep[:controls], w[:width, states:].T, 0.0)

    smem = pl.BlockSpec(memory_space=pltpu.SMEM)
    vmem = pl.BlockSpec(memory_space=pltpu.VMEM)
    return pl.pallas_call(
        body,
        name="iterate",
        out_shape=(
            jax.ShapeDtypeStruct((states, width), jnp.float32),
            jax.ShapeDtypeStruct((controls, width), jnp.float32),
            jax.ShapeDtypeStruct((states, width), jnp.float32),
            jax.ShapeDtypeStruct((parts, LANES), jnp.float32),
        ),
        in_specs=[smem, smem, vmem, vmem, vmem, vmem],
        out_specs=(vmem, vmem, vmem, vmem),
        scratch_shapes=[
            pltpu.VMEM((rows, both), jnp.float32),
            pltpu.VMEM((rows, both), jnp.float32),
            pltpu.VMEM((rows, states), jnp.float32),
            pltpu.VMEM((rows, states), jnp.float32),
            pltpu.VMEM((rows, states), jnp.float32),
            pltpu.VMEM((rows, states), jnp.bfloat16),
        ],
        compiler_params=pltpu.CompilerParams(vmem_limit_bytes=48 << 20),
    )(block_start, period, received, dynamics, gain, inverse)


def swap(rows, parts):
    flat = rows.reshape(parts, 1, rows.size // parts)
    return lax.all_to_all(flat, "section", 0, 0, tiled=True)


def local(dynamics, gain, inverse, lin_state, lin_input, block_start, period):
    parts = lax.axis_size("section")
    packed = pack(block_start, period, lin_state, lin_input, parts)
    received = swap(packed, parts).reshape(packed.shape)
    x, u, z, sums = iterate(block_start, period, received, dynamics, gain, inverse, parts)
    sums = swap(sums, parts)
    return x, u, z, jnp.sqrt(jnp.sum(sums[:, 0, :2], axis=0))


def solution(mesh):
    return jax.shard_map(
        local,
        mesh=mesh,
        in_specs=(
            P("plant", None),
            P("plant", None),
            P("plant", None),
            P(("plant", "section"), None),
            P(("plant", "section"), None),
            P("plant"),
            P("plant"),
        ),
        out_specs=(P("plant", "section"), P("plant", "section"), P("plant", "section"), P("plant")),
        check_vma=False,
    )
```

time: 181 us -> 66.4 us (0.37)
  starting transfers between devices: 66.5 us -> 0 us
  waiting for transfers between devices: 42.7 us -> 0 us
  blocking collectives: 27.2 us -> 54.3 us
  other arithmetic: 20 us -> 0.08 us
  local copies, waits for them, and re-layouts: 12 us -> 2.52 us
  Pallas kernels: 0 us -> 7.22 us
  matrix products: 7.13 us -> 0 us
  between operations: 3.84 us -> 1.96 us
    all_to_all x6 -> x0, starting transfers between devices: 44.5 us -> none  [the longest x5 38.5 us: copy_for_each(): lax.all_to_all(jnp.broadcast_to(shard[None], (length, *shard.shape)), axi...]
    all_to_all x6 -> x0, waiting for transfers between devices: 30.9 us -> none  [the longest x1 15.6 us: local(): lax.all_to_all(state_parts, 'section', split_axis=1, concat_axis=0, tiled...]
    all_to_all x1 -> x2, blocking collectives: 27.2 us -> 54.3 us  [swap(): return lax.all_to_all(flat, 'section', 0, 0, tiled=True)]
    ppermute x8 -> x0, starting transfers between devices: 22 us -> none  [the longest x4 14.1 us: padded(): lax.ppermute(tail, axis, [(i, (i + 1) % count) for i in range(count)])]
    ppermute x8 -> x0, waiting for transfers between devices: 11.8 us -> none  [the longest x4 11.8 us: padded(): lax.ppermute(head, axis, [((i + 1) % count, i) for i in range(count)])]
    reduce_sum x9 -> x1, other arithmetic: 8.33 us -> 0.08 us  [local(): return (x, u, z, jnp.sqrt(jnp.sum(sums[:, 0, :2], axis=0)))]
    pallas_call x0 -> x2, Pallas kernels: none -> 7.22 us  [the longest x1 6.55 us: iterate(): pl.pallas_call(body, name='iterate', out_shape=(jax.ShapeDtypeStruct((sta...]
    dot_general x18 -> x0, matrix products: 7.13 us -> none  [the longest x4 2.1 us: estimate_condition(): jnp.dot(control_gain_array, rounded[condition_lines:], preferred_element_...]
  transfers between devices with their start and end apart: 14 -> 0, of which waited for: 10 -> 0; matrix products, arithmetic and copies ran while one was open for 4% -> 0% of each run, Pallas kernels for 0% -> 0%
where the time goes in v1:
time: 66.4 us; the launch traced here: 66.1 us
  blocking collectives  54.3 us (82%)
  Pallas kernels  7.22 us (11%)
  local copies, waits for them, and re-layouts  2.52 us (4%)
  between operations  1.96 us (3%)
    all_to_all x2, blocking collectives, swap(): return lax.all_to_all(flat, 'section', 0, 0, tiled=True)  54.3 us
    pallas_call x1, Pallas kernels, iterate(): pl.pallas_call(body, name='iterate', out_shape=(jax.ShapeDtypeStruct((sta...  6.55 us
    unnamed x10, local copies, waits for them, and re-layouts  2 us

profile of v1, /device:TPU:1, one launch (start us, length us, event | category | flops | bytes accessed | tf_op | source)
XLA Modules:
  0.0 66.1 jit_solution(459752268314859390)
XLA Ops:
  1.9 0.0 copy-start.2
  1.9 1.0 %copy-done.2 = f32[8,16384]{1,0:T(8,128)S(1)} copy-done((f32[8,16384]{1,0:T(8,128)S(1)}, f32[8,16384]{1,0:T(8,128)}, u32[]{:S(2)}) %copy-start.2) | copy-done | bytes 524312
  3.0 0.0 copy-start.4
  3.0 0.9 %copy-done.4 = f32[4,16384]{1,0:T(4,128)S(1)} copy-done((f32[4,16384]{1,0:T(4,128)S(1)}, f32[4,16384]{1,0:T(4,128)}, u32[]{:S(2)}) %copy-start.4) | copy-done | bytes 262168
  3.9 0.0 copy-start.1
  3.9 0.7 %pack.1 = f32[1600,128]{1,0:T(8,128)S(1)} custom-call(s32[1]{0:T(128)S(6)} %copy.13.bs_ref, s32[1]{0:T(128)S(6)} %copy.14.pe_ref, f32[8,16384]{1,0:T(8,128)S(1)} %copy-done.2, f32[4,16384]{1,0:T(4,128)S(1)} %copy-done.4), custom_call_target="tpu_custom_call" | custom-call | tf_op jit(solution)/shard_map/pack/pallas_call | solution.py:79
  4.6 0.0 copy-start
  4.6 0.0 copy-start.3
  4.6 39.1 %all_to_all.10 = f32[64,1,3200]{2,1,0:T(1,128)S(1)} all-to-all(f32[64,1,3200]{2,1,0:T(1,128)S(1)} %bitcast.6), channel_id=1, replica_groups=mesh['plant'=8,'section'=64] {'section'}, dimensions={0} | all-to-all | bytes 1638400 | tf_op jit(solution)/shard_map/all_to_all | solution.py:215
  43.7 0.0 copy-done.1
  43.7 0.0 copy-done
  43.7 0.0 copy-done.3
  43.7 6.6 %iterate.1 = (f32[512,256]{1,0:T(8,128)}, f32[256,256]{1,0:T(8,128)}, f32[512,256]{1,0:T(8,128)}, f32[64,128]{1,0:T(8,128)S(1)}) custom-call(s32[1]{0:T(128)S(6)} %copy.13.bs_ref, s32[1]{0:T(128)S(6)} %copy.14.pe_ref, f32[1600,128]{1,0:T(8,128)S(1)} %bitcast.5, bf16[512,512]{1,0:T(8,128)(2,1)S(1)} %copy-done.1, bf16[512,256]{1,0:T(8,128)(2,1)S(1)} %copy-done.3, ...), custom_call_target="tpu_custom_call" | custom-call | tf_op jit(solution)/shard_map/iterate/pallas_call | solution.py:190
  50.2 15.2 %all_to_all.11 = f32[64,1,128]{2,1,0:T(1,128)S(1)} all-to-all(f32[64,1,128]{2,1,0:T(1,128)S(1)} %bitcast.7), channel_id=1, replica_groups=mesh['plant'=8,'section'=64] {'section'}, dimensions={0} | all-to-all | bytes 65536 | tf_op jit(solution)/shard_map/all_to_all | solution.py:215
  65.5 0.1 slice_reduce_fusion
  65.6 0.5 sqrt.3
Async XLA Ops:
  1.9 1.0 %copy-start.2 = (f32[8,16384]{1,0:T(8,128)S(1)}, f32[8,16384]{1,0:T(8,128)}, u32[]{:S(2)}) copy-start(f32[8,16384]{1,0:T(8,128)} %st_ref.1) | copy-start | bytes 1572868
  3.0 0.9 %copy-start.4 = (f32[4,16384]{1,0:T(4,128)S(1)}, f32[4,16384]{1,0:T(4,128)}, u32[]{:S(2)}) copy-start(f32[4,16384]{1,0:T(4,128)} %in_ref.1) | copy-start | bytes 786436
  3.9 39.8 %copy-start.1 = (bf16[512,512]{1,0:T(8,128)(2,1)S(1)}, bf16[512,512]{1,0:T(8,128)(2,1)}, u32[]{:S(2)}) copy-start(bf16[512,512]{1,0:T(8,128)(2,1)} %a_ref.1) | copy-start | bytes 1572868
  4.6 39.1 %copy-start = (bf16[768,768]{1,0:T(8,128)(2,1)S(1)}, bf16[768,768]{1,0:T(8,128)(2,1)}, u32[]{:S(2)}) copy-start(bf16[768,768]{1,0:T(8,128)(2,1)} %k_ref.1) | copy-start | bytes 3538948
  4.6 39.1 %copy-start.3 = (bf16[512,256]{1,0:T(8,128)(2,1)S(1)}, bf16[512,256]{1,0:T(8,128)(2,1)}, u32[]{:S(2)}) copy-start(bf16[512,256]{1,0:T(8,128)(2,1)} %b_ref.1) | copy-start | bytes 786436

commit v2 on v1

--- a/solution.py
+++ b/solution.py
@@ -18,21 +18,39 @@
     per = 2 * rows_state + 2 * rows_input + 1
     assert width == 2 * LANES and rows_state == 8 and rows_input == 4
 
-    def body(bs_ref, pe_ref, st_ref, in_ref, out_ref, flat_ref, halo_ref):
+    pieces = 2
+    piece = total // pieces
+
+    def body(bs_ref, pe_ref, st_hbm, in_hbm, out_ref, st_ref, in_ref, st_first, in_first, flat_ref, halo_ref, sems):
         bs = bs_ref[0]
         pe = pe_ref[0]
+        opening = pl.ds(pl.multiple_of(bs * width, LANES), LANES)
+        copies = [
+            pltpu.make_async_copy(st_hbm.at[:, opening], st_first, sems.at[0]),
+            pltpu.make_async_copy(in_hbm.at[:, opening], in_first, sems.at[1]),
+        ]
+        for q in range(pieces):
+            at = slice(piece * q, piece * q + piece)
+            copies.append(pltpu.make_async_copy(st_hbm.at[:, at], st_ref.at[:, at], sems.at[2 + 2 * q]))
+            copies.append(pltpu.make_async_copy(in_hbm.at[:, at], in_ref.at[:, at], sems.at[3 + 2 * q]))
+        for copy in copies:
+            copy.start()
         lane = lax.broadcasted_iota(jnp.int32, (16, LANES), 1)
+        spare = jnp.zeros((4, LANES), jnp.float32)
 
         def tile(position):
             at = pl.ds(pl.multiple_of(position, LANES), LANES)
-            return jnp.concatenate(
-                [st_ref[:, at], in_ref[:, at], jnp.zeros((4, LANES), jnp.float32)], axis=0
-            )
-
-        first = tile(bs * width)
+            return jnp.concatenate([st_ref[:, at], in_ref[:, at], spare], axis=0)
+
+        copies[0].wait()
+        copies[1].wait()
+        first = jnp.concatenate([st_first[...], in_first[...], spare], axis=0)
         onward = pltpu.roll(first, lax.rem(pe, LANES), 1)
         edges = []
         for q in range(4):
+            if q * pieces % 4 == 0:
+                copies[2 + 2 * (q * pieces // 4)].wait()
+                copies[3 + 2 * (q * pieces // 4)].wait()
             collected = jnp.zeros((16, LANES), jnp.float32)
             for e in range(16):
                 d = 16 * q + e
@@ -76,18 +94,29 @@
 
     smem = pl.BlockSpec(memory_space=pltpu.SMEM)
     vmem = pl.BlockSpec(memory_space=pltpu.VMEM)
+    hbm = pl.BlockSpec(memory_space=pltpu.HBM)
     return pl.pallas_call(
         body,
         name="pack",
         out_shape=jax.ShapeDtypeStruct((parts * per, LANES), jnp.float32),
-        in_specs=[smem, smem, vmem, vmem],
+        in_specs=[smem, smem, hbm, hbm],
         out_specs=vmem,
         scratch_shapes=[
+            pltpu.VMEM(state.shape, jnp.float32),
+            pltpu.VMEM(inputs.shape, jnp.float32),
+            pltpu.VMEM((rows_state, LANES), jnp.float32),
+            pltpu.VMEM((rows_input, LANES), jnp.float32),
             pltpu.VMEM((4 * LANES, LANES), jnp.float32),
             pltpu.VMEM((parts, LANES), jnp.float32),
+            pltpu.SemaphoreType.DMA((2 + 2 * pieces,)),
         ],
         compiler_params=pltpu.CompilerParams(vmem_limit_bytes=32 << 20),
-    )(block_start, period, state, inputs)
+    )(
+        block_start,
+        period,
+        pltpu.with_memory_space_constraint(state, pltpu.HBM),
+        pltpu.with_memory_space_constraint(inputs, pltpu.HBM),
+    )
 
 
 def iterate(block_start, period, received, dynamics, gain, inverse, parts):
@@ -191,10 +220,10 @@
         body,
         name="iterate",
         out_shape=(
-            jax.ShapeDtypeStruct((states, width), jnp.float32),
-            jax.ShapeDtypeStruct((controls, width), jnp.float32),
-            jax.ShapeDtypeStruct((states, width), jnp.float32),
-            jax.ShapeDtypeStruct((parts, LANES), jnp.float32),
+            pltpu.VMEM((states, width), jnp.float32),
+            pltpu.VMEM((controls, width), jnp.float32),
+            pltpu.VMEM((states, width), jnp.float32),
+            pltpu.VMEM((parts, LANES), jnp.float32),
         ),
         in_specs=[smem, smem, vmem, vmem, vmem, vmem],
         out_specs=(vmem, vmem, vmem, vmem),

time: 66.4 us -> 65.4 us (0.985)
  blocking collectives: 54.3 us -> 39.1 us
  waiting for transfers between devices: 0 us -> 7.31 us
  starting transfers between devices: 0 us -> 5.86 us
  Pallas kernels: 7.22 us -> 8.11 us
    all_to_all x2 -> x1, blocking collectives: 54.3 us -> 39.1 us  [swap(): return lax.all_to_all(flat, 'section', 0, 0, tiled=True)]
    all_to_all x0 -> x1, waiting for transfers between devices: none -> 7.31 us  [swap(): return lax.all_to_all(flat, 'section', 0, 0, tiled=True)]
    all_to_all x0 -> x1, starting transfers between devices: none -> 5.86 us  [swap(): return lax.all_to_all(flat, 'section', 0, 0, tiled=True)]
    pallas_call x1, Pallas kernels: 0.67 us -> 1.85 us  [pack(): pl.pallas_call(body, name='pack', out_shape=jax.ShapeDtypeStruct((parts *...]
    unnamed x10 -> x9, local copies, waits for them, and re-layouts: 2 us -> 2.31 us
  transfers between devices with their start and end apart: 0 -> 1, of which waited for: 0 -> 1; matrix products, arithmetic and copies ran while one was open for 0% -> 4% of each run, Pallas kernels for 0% -> 0%
where the time goes in v2:
time: 65.4 us; the launch traced here: 65.2 us
  blocking collectives  39.1 us (60%)
  Pallas kernels  8.11 us (12%)
  waiting for transfers between devices  7.31 us (11%)
  starting transfers between devices  5.86 us (9%)
  local copies, waits for them, and re-layouts  2.83 us (4%)
  between operations  1.97 us (3%)
    all_to_all x1, blocking collectives, swap(): return lax.all_to_all(flat, 'section', 0, 0, tiled=True)  39.1 us
    all_to_all x1, waiting for transfers between devices, swap(): return lax.all_to_all(flat, 'section', 0, 0, tiled=True)  7.31 us
    pallas_call x1, Pallas kernels, iterate(): pl.pallas_call(body, name='iterate', out_shape=(pltpu.VMEM((states, width...  6.26 us
    all_to_all x1, starting transfers between devices, swap(): return lax.all_to_all(flat, 'section', 0, 0, tiled=True)  5.86 us
    unnamed x9, local copies, waits for them, and re-layouts  2.31 us
    pallas_call x1, Pallas kernels, pack(): pl.pallas_call(body, name='pack', out_shape=jax.ShapeDtypeStruct((parts *...  1.85 us
  transfers between devices with their start and end apart: 1, of which 1 were waited for; matrix products, arithmetic and copies ran while one was open for 4% of the time, Pallas kernels for 0%

profile of v2, /device:TPU:1, one launch (start us, length us, event | category | flops | bytes accessed | tf_op | source)
XLA Modules:
  0.0 65.2 jit_solution(5926365472782912878)
XLA Ops:
  1.9 0.0 copy-start.1
  1.9 1.9 %pack.1 = f32[1600,128]{1,0:T(8,128)S(1)} custom-call(s32[1]{0:T(128)S(6)} %copy.16.bs_ref, s32[1]{0:T(128)S(6)} %copy.17.pe_ref, f32[8,16384]{1,0:T(8,128)} %st_hbm.1, f32[4,16384]{1,0:T(4,128)} %in_hbm.1), custom_call_target="tpu_custom_call" | custom-call | tf_op jit(solution)/shard_map/pack/pallas_call | solution.py:98
  3.8 0.0 copy-start
  3.8 0.0 copy-start.2
  3.8 39.1 %all_to_all.10 = f32[64,1,3200]{2,1,0:T(1,128)S(1)} all-to-all(f32[64,1,3200]{2,1,0:T(1,128)S(1)} %bitcast.6), channel_id=1, replica_groups=mesh['plant'=8,'section'=64] {'section'}, dimensions={0} | all-to-all | bytes 1638400 | tf_op jit(solution)/shard_map/all_to_all | solution.py:244
  42.9 0.0 copy-done.1
  42.9 0.0 copy-done
  42.9 0.0 copy-done.2
  42.9 6.3 %iterate.1 = (f32[512,256]{1,0:T(8,128)S(1)}, f32[256,256]{1,0:T(8,128)S(1)}, f32[512,256]{1,0:T(8,128)S(1)}, f32[64,128]{1,0:T(8,128)}) custom-call(s32[1]{0:T(128)S(6)} %copy.16.bs_ref, s32[1]{0:T(128)S(6)} %copy.17.pe_ref, f32[1600,128]{1,0:T(8,128)S(1)} %bitcast.5, bf16[512,512]{1,0:T(8,128)(2,1)S(1)} %copy-done.1, bf16[512,256]{1,0:T(8,128)(2,1)S(1)} %copy-done.2, ...), custom_call_target="tpu_custom_call" | custom-call | tf_op jit(solution)/shard_map/iterate/pallas_call | solution.py:219
  49.1 5.9 %all-to-all-start.1 = ((f32[64,1,128]{2,1,0:T(1,128)}), f32[64,1,128]{2,1,0:T(1,128)S(1)}, u32[]{:S(2)}, u32[]{:S(2)}) async-start(f32[64,1,128]{2,1,0:T(1,128)} %bitcast.3), calls=%async_computation.1 | async-start | bytes 65536 | tf_op jit(solution)/shard_map/all_to_all | solution.py:244
  55.0 0.8 %copy.13 = f32[512,256]{1,0:T(8,128)} copy(f32[512,256]{1,0:T(8,128)S(1)} %get-tuple-element.12) | data formatting | bytes 1048576
  55.8 0.7 %copy.14 = f32[256,256]{1,0:T(8,128)} copy(f32[256,256]{1,0:T(8,128)S(1)} %get-tuple-element.13) | data formatting | bytes 524288
  56.5 0.8 %copy.15 = f32[512,256]{1,0:T(8,128)} copy(f32[512,256]{1,0:T(8,128)S(1)} %get-tuple-element.14) | data formatting | bytes 1048576
  57.3 7.3 %all-to-all-done.1 = f32[64,1,128]{2,1,0:T(1,128)S(1)} async-done(((f32[64,1,128]{2,1,0:T(1,128)}), f32[64,1,128]{2,1,0:T(1,128)S(1)}, u32[]{:S(2)}, u32[]{:S(2)}) %all-to-all-start.1) | async-done | bytes 32800 | tf_op jit(solution)/shard_map/all_to_all | solution.py:244
  64.6 0.1 slice_reduce_fusion
  64.7 0.5 sqrt.3
Async XLA Ops:
  1.9 41.0 %copy-start.1 = (bf16[512,512]{1,0:T(8,128)(2,1)S(1)}, bf16[512,512]{1,0:T(8,128)(2,1)}, u32[]{:S(2)}) copy-start(bf16[512,512]{1,0:T(8,128)(2,1)} %a_ref.1) | copy-start | bytes 1572868
  3.8 39.1 %copy-start = (bf16[768,768]{1,0:T(8,128)(2,1)S(1)}, bf16[768,768]{1,0:T(8,128)(2,1)}, u32[]{:S(2)}) copy-start(bf16[768,768]{1,0:T(8,128)(2,1)} %k_ref.1) | copy-start | bytes 3538948
  3.8 39.1 %copy-start.2 = (bf16[512,256]{1,0:T(8,128)(2,1)S(1)}, bf16[512,256]{1,0:T(8,128)(2,1)}, u32[]{:S(2)}) copy-start(bf16[512,256]{1,0:T(8,128)(2,1)} %b_ref.1) | copy-start | bytes 786436
  49.1 15.5 %all-to-all-start.1 = ((f32[64,1,128]{2,1,0:T(1,128)}), f32[64,1,128]{2,1,0:T(1,128)S(1)}, u32[]{:S(2)}, u32[]{:S(2)}) async-start(f32[64,1,128]{2,1,0:T(1,128)} %bitcast.3), calls=%async_computation.1 | async-start | bytes 65536 | tf_op jit(solution)/shard_map/all_to_all | solution.py:244

commit v3 on v2

--- a/solution.py
+++ b/solution.py
@@ -125,13 +125,14 @@
     both = states + controls
     width = 2 * LANES
     rows = width + 2 * HALO
+    span = states
     per = received.shape[0] // parts
     nt = (((1,), (1,)), ((), ()))
     nn = (((1,), (0,)), ((), ()))
     tn = (((0,), (0,)), ((), ()))
 
     def body(bs_ref, pe_ref, got_ref, a_ref, b_ref, k_ref, x_ref, u_ref, z_ref, sums_ref,
-             neg_ref, w_ref, zs_ref, ys_ref, vs_ref, gn_ref):
+             neg_ref, nd_ref, zs_ref, ys_ref, vs_ref, gn_ref, ab_ref):
         sub = lax.broadcasted_iota(jnp.int32, (8, LANES), 0)
         for g in range(states // LANES):
             for j in range(2):
@@ -166,53 +167,61 @@
         wide = jnp.where(slot == place, wide, 0.0).reshape(8, 16, both).sum(axis=1)
         neg_ref[width : width + 8, :] = -pltpu.roll(wide, HALO, 0)
 
+        ab_ref[:, :states] = a_ref[...]
+        ab_ref[:, states:] = b_ref[...]
         for it in range(ITERS):
             last = it == ITERS - 1
             if it == 0:
                 rhs = neg_ref[...].astype(jnp.bfloat16)
             else:
                 g = gn_ref[...]
-                t_s = lax.dot_general(g, a_ref[...], nn, preferred_element_type=jnp.float32)
-                t_u = lax.dot_general(g, b_ref[...], nn, preferred_element_type=jnp.float32)
+                t = lax.dot_general(g, ab_ref[...], nn, preferred_element_type=jnp.float32)
                 rhs = jnp.concatenate(
                     [
-                        (neg_ref[:, :states] + RHO * (zs_ref[...] - ys_ref[...]) + RHO * t_s).astype(jnp.bfloat16),
-                        (neg_ref[:, states:] + RHO * t_u).astype(jnp.bfloat16),
+                        (nd_ref[...] + RHO * t[:, :states]).astype(jnp.bfloat16),
+                        (neg_ref[:, states:] + RHO * t[:, states:]).astype(jnp.bfloat16),
                     ],
                     axis=1,
                 )
             w = lax.dot_general(rhs, k_ref[...], nt, preferred_element_type=jnp.float32)
-            x = w[:, :states]
             wb = w.astype(jnp.bfloat16)
-            pred = lax.dot_general(wb[:, :states], a_ref[...], nt, preferred_element_type=jnp.float32)
-            pred = pred + lax.dot_general(wb[:, states:], b_ref[...], nt, preferred_element_type=jnp.float32)
-            if it == 0:
-                a, p = x, pred
-            else:
-                a, p = x + ys_ref[...], pred + vs_ref[...]
-            znew = 0.5 * (a + pltpu.roll(p, 1, 0))
-            znn = pltpu.roll(znew, rows - 1, 0)
-            if not last:
-                ys_ref[...] = a - znew
-                v = p - znn
-                vs_ref[...] = v
-                gn_ref[...] = (znn - v).astype(jnp.bfloat16)
-                zs_ref[...] = znew
-            else:
+            primal, dual = 0.0, 0.0
+            if last:
                 idx = lax.rem(lax.axis_index("section") - bs_ref[0] + parts, parts)
                 count = pe_ref[0] - idx * width
-                here = lax.broadcasted_iota(jnp.int32, (width, states), 0) < count
-                gap = (x - znew)[:width]
-                miss = (pred - znn)[:width]
-                step = znew[:width] - zs_ref[:width, :]
-                primal = jnp.sum(jnp.where(here, gap * gap + miss * miss, 0.0))
-                dual = RHO * RHO * jnp.sum(jnp.where(here, step * step, 0.0))
+                here = lax.broadcasted_iota(jnp.int32, (width, span), 0) < count
+                keep = lax.broadcasted_iota(jnp.int32, (states, width), 1) < count
+                u_ref[...] = jnp.where(keep[:controls], w[:width, states:].T, 0.0)
+            for n in range(0, states, span):
+                at = slice(n, n + span)
+                x = w[:, at]
+                pred = lax.dot_general(wb, ab_ref[at, :], nt, preferred_element_type=jnp.float32)
+                if it == 0:
+                    a, p = x, pred
+                else:
+                    a, p = x + ys_ref[:, at], pred + vs_ref[:, at]
+                znew = 0.5 * (a + pltpu.roll(p, 1, 0))
+                znn = pltpu.roll(znew, rows - 1, 0)
+                if not last:
+                    y = a - znew
+                    v = p - znn
+                    ys_ref[:, at] = y
+                    vs_ref[:, at] = v
+                    gn_ref[:, at] = (znn - v).astype(jnp.bfloat16)
+                    nd_ref[:, at] = neg_ref[:, at] + RHO * (znew - y)
+                    if it == ITERS - 2:
+                        zs_ref[:, at] = znew[:width]
+                else:
+                    gap = (x - znew)[:width]
+                    miss = (pred - znn)[:width]
+                    step = znew[:width] - zs_ref[:, at]
+                    primal += jnp.sum(jnp.where(here, gap * gap + miss * miss, 0.0), axis=0, keepdims=True)
+                    dual += RHO * RHO * jnp.sum(jnp.where(here, step * step, 0.0), axis=0, keepdims=True)
+                    x_ref[at, :] = jnp.where(keep[at], x[:width].T, 0.0)
+                    z_ref[at, :] = jnp.where(keep[at], znew[:width].T, 0.0)
+            if last:
                 lane = lax.broadcasted_iota(jnp.int32, (parts, LANES), 1)
-                sums_ref[...] = jnp.where(lane == 0, primal, jnp.where(lane == 1, dual, 0.0))
-                keep = lax.broadcasted_iota(jnp.int32, (states, width), 1) < count
-                x_ref[...] = jnp.where(keep, x[:width].T, 0.0)
-                z_ref[...] = jnp.where(keep, znew[:width].T, 0.0)
-                u_ref[...] = jnp.where(keep[:controls], w[:width, states:].T, 0.0)
+                sums_ref[...] = jnp.where(lane == 0, jnp.sum(primal), jnp.where(lane == 1, jnp.sum(dual), 0.0))
 
     smem = pl.BlockSpec(memory_space=pltpu.SMEM)
     vmem = pl.BlockSpec(memory_space=pltpu.VMEM)
@@ -229,11 +238,12 @@
         out_specs=(vmem, vmem, vmem, vmem),
         scratch_shapes=[
             pltpu.VMEM((rows, both), jnp.float32),
-            pltpu.VMEM((rows, both), jnp.float32),
             pltpu.VMEM((rows, states), jnp.float32),
+            pltpu.VMEM((width, states), jnp.float32),
             pltpu.VMEM((rows, states), jnp.float32),
             pltpu.VMEM((rows, states), jnp.float32),
             pltpu.VMEM((rows, states), jnp.bfloat16),
+            pltpu.VMEM((states, both), jnp.bfloat16),
         ],
         compiler_params=pltpu.CompilerParams(vmem_limit_bytes=48 << 20),
     )(block_start, period, received, dynamics, gain, inverse)

time: 65.4 us -> 64.4 us (0.985)
  Pallas kernels: 8.11 us -> 7.09 us
    pallas_call x1, Pallas kernels: 6.26 us -> 5.24 us  [iterate(): pl.pallas_call(body, name='iterate', out_shape=(pltpu.VMEM((states, width...]
where the time goes in v3:
time: 64.4 us; the launch traced here: 64.2 us
  blocking collectives  39.1 us (61%)
  waiting for transfers between devices  7.31 us (11%)
  Pallas kernels  7.09 us (11%)
  starting transfers between devices  5.87 us (9%)
  local copies, waits for them, and re-layouts  2.83 us (4%)
  between operations  1.97 us (3%)
    all_to_all x1, blocking collectives, swap(): return lax.all_to_all(flat, 'section', 0, 0, tiled=True)  39.1 us
    all_to_all x1, waiting for transfers between devices, swap(): return lax.all_to_all(flat, 'section', 0, 0, tiled=True)  7.31 us
    all_to_all x1, starting transfers between devices, swap(): return lax.all_to_all(flat, 'section', 0, 0, tiled=True)  5.87 us
    pallas_call x1, Pallas kernels, iterate(): pl.pallas_call(body, name='iterate', out_shape=(pltpu.VMEM((states, width...  5.24 us
    unnamed x9, local copies, waits for them, and re-layouts  2.31 us
    pallas_call x1, Pallas kernels, pack(): pl.pallas_call(body, name='pack', out_shape=jax.ShapeDtypeStruct((parts *...  1.85 us
  transfers between devices with their start and end apart: 1, of which 1 were waited for; matrix products, arithmetic and copies ran while one was open for 4% of the time, Pallas kernels for 0%

profile of v3, /device:TPU:1, one launch (start us, length us, event | category | flops | bytes accessed | tf_op | source)
XLA Modules:
  0.0 64.2 jit_solution(745219761995341561)
XLA Ops:
  1.9 0.0 copy-start.1
  1.9 1.9 %pack.1 = f32[1600,128]{1,0:T(8,128)S(1)} custom-call(s32[1]{0:T(128)S(6)} %copy.16.bs_ref, s32[1]{0:T(128)S(6)} %copy.17.pe_ref, f32[8,16384]{1,0:T(8,128)} %st_hbm.1, f32[4,16384]{1,0:T(4,128)} %in_hbm.1), custom_call_target="tpu_custom_call" | custom-call | tf_op jit(solution)/shard_map/pack/pallas_call | solution.py:98
  3.8 0.0 copy-start
  3.8 0.0 copy-start.2
  3.8 39.1 %all_to_all.10 = f32[64,1,3200]{2,1,0:T(1,128)S(1)} all-to-all(f32[64,1,3200]{2,1,0:T(1,128)S(1)} %bitcast.6), channel_id=1, replica_groups=mesh['plant'=8,'section'=64] {'section'}, dimensions={0} | all-to-all | bytes 1638400 | tf_op jit(solution)/shard_map/all_to_all | solution.py:254
  42.9 0.0 copy-done.1
  42.9 0.0 copy-done
  42.9 0.0 copy-done.2
  42.9 5.2 %iterate.1 = (f32[512,256]{1,0:T(8,128)S(1)}, f32[256,256]{1,0:T(8,128)S(1)}, f32[512,256]{1,0:T(8,128)S(1)}, f32[64,128]{1,0:T(8,128)}) custom-call(s32[1]{0:T(128)S(6)} %copy.16.bs_ref, s32[1]{0:T(128)S(6)} %copy.17.pe_ref, f32[1600,128]{1,0:T(8,128)S(1)} %bitcast.5, bf16[512,512]{1,0:T(8,128)(2,1)S(1)} %copy-done.1, bf16[512,256]{1,0:T(8,128)(2,1)S(1)} %copy-done.2, ...), custom_call_target="tpu_custom_call" | custom-call | tf_op jit(solution)/shard_map/iterate/pallas_call | solution.py:228
  48.1 5.9 %all-to-all-start.1 = ((f32[64,1,128]{2,1,0:T(1,128)}), f32[64,1,128]{2,1,0:T(1,128)S(1)}, u32[]{:S(2)}, u32[]{:S(2)}) async-start(f32[64,1,128]{2,1,0:T(1,128)} %bitcast.3), calls=%async_computation.1 | async-start | bytes 65536 | tf_op jit(solution)/shard_map/all_to_all | solution.py:254
  54.0 0.8 %copy.13 = f32[512,256]{1,0:T(8,128)} copy(f32[512,256]{1,0:T(8,128)S(1)} %get-tuple-element.12) | data formatting | bytes 1048576
  54.8 0.7 %copy.14 = f32[256,256]{1,0:T(8,128)} copy(f32[256,256]{1,0:T(8,128)S(1)} %get-tuple-element.13) | data formatting | bytes 524288
  55.5 0.8 %copy.15 = f32[512,256]{1,0:T(8,128)} copy(f32[512,256]{1,0:T(8,128)S(1)} %get-tuple-element.14) | data formatting | bytes 1048576
  56.3 7.3 %all-to-all-done.1 = f32[64,1,128]{2,1,0:T(1,128)S(1)} async-done(((f32[64,1,128]{2,1,0:T(1,128)}), f32[64,1,128]{2,1,0:T(1,128)S(1)}, u32[]{:S(2)}, u32[]{:S(2)}) %all-to-all-start.1) | async-done | bytes 32800 | tf_op jit(solution)/shard_map/all_to_all | solution.py:254
  63.6 0.1 slice_reduce_fusion
  63.7 0.5 sqrt.3
Async XLA Ops:
  1.9 41.0 %copy-start.1 = (bf16[512,512]{1,0:T(8,128)(2,1)S(1)}, bf16[512,512]{1,0:T(8,128)(2,1)}, u32[]{:S(2)}) copy-start(bf16[512,512]{1,0:T(8,128)(2,1)} %a_ref.1) | copy-start | bytes 1572868
  3.8 39.1 %copy-start = (bf16[768,768]{1,0:T(8,128)(2,1)S(1)}, bf16[768,768]{1,0:T(8,128)(2,1)}, u32[]{:S(2)}) copy-start(bf16[768,768]{1,0:T(8,128)(2,1)} %k_ref.1) | copy-start | bytes 3538948
  3.8 39.1 %copy-start.2 = (bf16[512,256]{1,0:T(8,128)(2,1)S(1)}, bf16[512,256]{1,0:T(8,128)(2,1)}, u32[]{:S(2)}) copy-start(bf16[512,256]{1,0:T(8,128)(2,1)} %b_ref.1) | copy-start | bytes 786436
  48.1 15.5 %all-to-all-start.1 = ((f32[64,1,128]{2,1,0:T(1,128)}), f32[64,1,128]{2,1,0:T(1,128)S(1)}, u32[]{:S(2)}, u32[]{:S(2)}) async-start(f32[64,1,128]{2,1,0:T(1,128)} %bitcast.3), calls=%async_computation.1 | async-start | bytes 65536 | tf_op jit(solution)/shard_map/all_to_all | solution.py:254

commit v4 on v3

--- a/solution.py
+++ b/solution.py
@@ -21,7 +21,7 @@
     pieces = 2
     piece = total // pieces
 
-    def body(bs_ref, pe_ref, st_hbm, in_hbm, out_ref, st_ref, in_ref, st_first, in_first, flat_ref, halo_ref, sems):
+    def body(bs_ref, pe_ref, st_hbm, in_hbm, out_ref, st_ref, in_ref, st_first, in_first, flat_ref, sems):
         bs = bs_ref[0]
         pe = pe_ref[0]
         opening = pl.ds(pl.multiple_of(bs * width, LANES), LANES)
@@ -78,15 +78,22 @@
         skip = total - pe
         skip = jnp.where(skip < HALO, skip, 0)
         head = pltpu.roll(first, lax.rem(8 * lax.rem(bs, 16) + HALO - skip + LANES, LANES), 1)
+        values = []
         for q in range(4):
             block = 16 * q + (lane >> 3)
             slot = lane & 7
             value = jnp.where((block == before) & (slot < HALO), tail, edges[q])
-            value = jnp.where((block == bs) & (slot >= HALO), head, value)
-            flat_ref[LANES * q : LANES * q + LANES, 0:16] = value.T
+            values.append(jnp.where((block == bs) & (slot >= HALO), head, value))
+        flat_ref[:, 0:64] = jnp.concatenate(values, axis=0).T
+        parts_of = [jnp.zeros((16, LANES), jnp.float32)] * 4
+        lane16 = lane[:16]
         for h in range(8):
-            halo_ref[:, 16 * h : 16 * h + 16] = flat_ref[pl.ds(h, parts, stride=8), 0:16]
-        flat = halo_ref[...]
+            picked = flat_ref[pl.ds(h, 16, stride=8), :]
+            for q in range(4):
+                shift = (16 * h - 16 * q) % LANES
+                moved = pltpu.roll(picked, shift, 1) if shift else picked
+                parts_of[q] = jnp.where((lane16 >> 4) == h, moved, parts_of[q])
+        flat = jnp.concatenate(parts_of, axis=0)
         lane = lax.broadcasted_iota(jnp.int32, (parts, LANES), 1)
         out_ref[pl.ds(per - 1, parts, stride=per), :] = jnp.where(
             lane < 64, pltpu.roll(flat, 1, 0), pltpu.roll(flat, parts - 1, 0)
@@ -106,8 +113,7 @@
             pltpu.VMEM(inputs.shape, jnp.float32),
             pltpu.VMEM((rows_state, LANES), jnp.float32),
             pltpu.VMEM((rows_input, LANES), jnp.float32),
-            pltpu.VMEM((4 * LANES, LANES), jnp.float32),
-            pltpu.VMEM((parts, LANES), jnp.float32),
+            pltpu.VMEM((LANES, LANES), jnp.float32),
             pltpu.SemaphoreType.DMA((2 + 2 * pieces,)),
         ],
         compiler_params=pltpu.CompilerParams(vmem_limit_bytes=32 << 20),
@@ -126,20 +132,54 @@
     width = 2 * LANES
     rows = width + 2 * HALO
     span = states
+    run = width // 8
     per = received.shape[0] // parts
     nt = (((1,), (1,)), ((), ()))
     nn = (((1,), (0,)), ((), ()))
     tn = (((0,), (0,)), ((), ()))
 
     def body(bs_ref, pe_ref, got_ref, a_ref, b_ref, k_ref, x_ref, u_ref, z_ref, sums_ref,
-             neg_ref, nd_ref, zs_ref, ys_ref, vs_ref, gn_ref, ab_ref):
+             nd_ref, ys_ref, vs_ref, gn_ref, ab_ref, *tiled):
+        tiles = states // LANES
+        neg_refs = tiled[: both // LANES]
+        ws_refs = tiled[both // LANES : 2 * both // LANES]
+        zs_refs = tiled[2 * both // LANES :]
         sub = lax.broadcasted_iota(jnp.int32, (8, LANES), 0)
+        edge_row = lax.broadcasted_iota(jnp.int32, (8, states), 0)
+
+        def lay(half, at, columns):
+            for i in range(LANES // run):
+                to = pl.ds(half * (LANES // run) + i, run, stride=8)
+                neg_refs[at // LANES][to, :] = columns[run * i : run * i + run]
+
+        def in_order(ref):
+            return jnp.concatenate([ref[pl.ds(i, run, stride=8), :] for i in range(8)], axis=0)
+
+        def keep_in(refs, values):
+            for k, ref in enumerate(refs):
+                ref[...] = values[:width, LANES * k : LANES * k + LANES]
+
+        def joined(refs):
+            return jnp.concatenate([ref[...] for ref in refs], axis=1)
+
+        def back(values):
+            near = pltpu.roll(values[width - 8 : width], 1, 0)
+            halo = pltpu.roll(values[width:], 1, 0)
+            begin = jnp.where(edge_row == 0, halo, near)
+            return jnp.concatenate([begin, values[: width - 8], jnp.where(edge_row == 0, near, halo)], axis=0)
+
+        def onward(values):
+            near = pltpu.roll(values[:8], 7, 0)
+            halo = pltpu.roll(values[width:], 7, 0)
+            end = jnp.where(edge_row == 7, halo, near)
+            return jnp.concatenate([values[8:width], end, jnp.where(edge_row == 7, near, halo)], axis=0)
+
         for g in range(states // LANES):
             for j in range(2):
                 block = jnp.concatenate(
                     [got_ref[per * s + 8 * j : per * s + 8 * j + 8, :] for s in range(16 * g, 16 * g + 16)], axis=0
                 )
-                neg_ref[LANES * j : LANES * j + LANES, LANES * g : LANES * g + LANES] = -block.T
+                lay(j, LANES * g, -block.T)
         for g in range(controls // LANES):
             halves = ([], [])
             for s in range(32 * g, 32 * g + 32, 2):
@@ -149,7 +189,7 @@
                 halves[1].append(jnp.where(sub < 4, pltpu.roll(one, 4, 0), two))
             for j in range(2):
                 at = states + LANES * g
-                neg_ref[LANES * j : LANES * j + LANES, at : at + LANES] = -jnp.concatenate(halves[j], axis=0).T
+                lay(j, at, -jnp.concatenate(halves[j], axis=0).T)
         edge = got_ref[pl.ds(per - 1, parts, stride=per), :]
         high = edge.astype(jnp.bfloat16)
         rest = edge - high.astype(jnp.float32)
@@ -165,21 +205,23 @@
         col = lax.broadcasted_iota(jnp.int32, (LANES, both), 1)
         place = jnp.where(col < states, col & 7, 8 + (col & 3))
         wide = jnp.where(slot == place, wide, 0.0).reshape(8, 16, both).sum(axis=1)
-        neg_ref[width : width + 8, :] = -pltpu.roll(wide, HALO, 0)
+        wide = -pltpu.roll(wide, HALO, 0)
+        for k, ref in enumerate(neg_refs):
+            ref[width : width + 8, :] = wide[:, LANES * k : LANES * k + LANES]
 
         ab_ref[:, :states] = a_ref[...]
         ab_ref[:, states:] = b_ref[...]
         for it in range(ITERS):
             last = it == ITERS - 1
             if it == 0:
-                rhs = neg_ref[...].astype(jnp.bfloat16)
+                rhs = joined(neg_refs).astype(jnp.bfloat16)
             else:
                 g = gn_ref[...]
                 t = lax.dot_general(g, ab_ref[...], nn, preferred_element_type=jnp.float32)
                 rhs = jnp.concatenate(
                     [
                         (nd_ref[...] + RHO * t[:, :states]).astype(jnp.bfloat16),
-                        (neg_ref[:, states:] + RHO * t[:, states:]).astype(jnp.bfloat16),
+                        (joined(neg_refs[tiles:]) + RHO * t[:, states:]).astype(jnp.bfloat16),
                     ],
                     axis=1,
                 )
@@ -189,9 +231,12 @@
             if last:
                 idx = lax.rem(lax.axis_index("section") - bs_ref[0] + parts, parts)
                 count = pe_ref[0] - idx * width
-                here = lax.broadcasted_iota(jnp.int32, (width, span), 0) < count
-                keep = lax.broadcasted_iota(jnp.int32, (states, width), 1) < count
-                u_ref[...] = jnp.where(keep[:controls], w[:width, states:].T, 0.0)
+                row = lax.broadcasted_iota(jnp.int32, (width, span), 0)
+                here = run * (row & 7) + (row >> 3) < count
+                keep = lax.broadcasted_iota(jnp.int32, (LANES, width), 1) < count
+                keep_in(ws_refs, w)
+                for k in range(controls // LANES):
+                    u_ref[LANES * k : LANES * k + LANES, :] = jnp.where(keep, in_order(ws_refs[tiles + k]).T, 0.0)
             for n in range(0, states, span):
                 at = slice(n, n + span)
                 x = w[:, at]
@@ -200,25 +245,28 @@
                     a, p = x, pred
                 else:
                     a, p = x + ys_ref[:, at], pred + vs_ref[:, at]
-                znew = 0.5 * (a + pltpu.roll(p, 1, 0))
-                znn = pltpu.roll(znew, rows - 1, 0)
+                znew = 0.5 * (a + back(p))
+                znn = onward(znew)
                 if not last:
                     y = a - znew
                     v = p - znn
                     ys_ref[:, at] = y
                     vs_ref[:, at] = v
                     gn_ref[:, at] = (znn - v).astype(jnp.bfloat16)
-                    nd_ref[:, at] = neg_ref[:, at] + RHO * (znew - y)
+                    nd_ref[:, at] = joined(neg_refs[:tiles]) + RHO * (znew - y)
                     if it == ITERS - 2:
-                        zs_ref[:, at] = znew[:width]
+                        keep_in(zs_refs, znew)
                 else:
                     gap = (x - znew)[:width]
                     miss = (pred - znn)[:width]
-                    step = znew[:width] - zs_ref[:, at]
+                    step = znew[:width] - joined(zs_refs)
                     primal += jnp.sum(jnp.where(here, gap * gap + miss * miss, 0.0), axis=0, keepdims=True)
                     dual += RHO * RHO * jnp.sum(jnp.where(here, step * step, 0.0), axis=0, keepdims=True)
-                    x_ref[at, :] = jnp.where(keep[at], x[:width].T, 0.0)
-                    z_ref[at, :] = jnp.where(keep[at], znew[:width].T, 0.0)
+                    keep_in(zs_refs, znew)
+                    for k in range(tiles):
+                        to = slice(LANES * k, LANES * k + LANES)
+                        x_ref[to, :] = jnp.where(keep, in_order(ws_refs[k]).T, 0.0)
+                        z_ref[to, :] = jnp.where(keep, in_order(zs_refs[k]).T, 0.0)
             if last:
                 lane = lax.broadcasted_iota(jnp.int32, (parts, LANES), 1)
                 sums_ref[...] = jnp.where(lane == 0, jnp.sum(primal), jnp.where(lane == 1, jnp.sum(dual), 0.0))
@@ -237,13 +285,13 @@
         in_specs=[smem, smem, vmem, vmem, vmem, vmem],
         out_specs=(vmem, vmem, vmem, vmem),
         scratch_shapes=[
-            pltpu.VMEM((rows, both), jnp.float32),
             pltpu.VMEM((rows, states), jnp.float32),
-            pltpu.VMEM((width, states), jnp.float32),
             pltpu.VMEM((rows, states), jnp.float32),
             pltpu.VMEM((rows, states), jnp.float32),
             pltpu.VMEM((rows, states), jnp.bfloat16),
             pltpu.VMEM((states, both), jnp.bfloat16),
+            *[pltpu.VMEM((rows, LANES), jnp.float32)] * (both // LANES),
+            *[pltpu.VMEM((width, LANES), jnp.float32)] * ((both + states) // LANES),
         ],
         compiler_params=pltpu.CompilerParams(vmem_limit_bytes=48 << 20),
     )(block_start, period, received, dynamics, gain, inverse)

time: 64.4 us -> 64 us (level)
  no operation moved by 1% of the time
where the time goes in v4:
time: 64 us; the launch traced here: 63.8 us
  blocking collectives  39.1 us (61%)
  waiting for transfers between devices  7.31 us (11%)
  Pallas kernels  6.69 us (10%)
  starting transfers between devices  5.86 us (9%)
  local copies, waits for them, and re-layouts  2.83 us (4%)
  between operations  1.97 us (3%)
    all_to_all x1, blocking collectives, swap(): return lax.all_to_all(flat, 'section', 0, 0, tiled=True)  39.1 us
    all_to_all x1, waiting for transfers between devices, swap(): return lax.all_to_all(flat, 'section', 0, 0, tiled=True)  7.31 us
    all_to_all x1, starting transfers between devices, swap(): return lax.all_to_all(flat, 'section', 0, 0, tiled=True)  5.86 us
    pallas_call x1, Pallas kernels, iterate(): pl.pallas_call(body, name='iterate', out_shape=(pltpu.VMEM((states, width...  4.88 us
    unnamed x9, local copies, waits for them, and re-layouts  2.31 us
    pallas_call x1, Pallas kernels, pack(): pl.pallas_call(body, name='pack', out_shape=jax.ShapeDtypeStruct((parts *...  1.81 us
  transfers between devices with their start and end apart: 1, of which 1 were waited for; matrix products, arithmetic and copies ran while one was open for 4% of the time, Pallas kernels for 0%

profile of v4, /device:TPU:1, one launch (start us, length us, event | category | flops | bytes accessed | tf_op | source)
XLA Modules:
  0.0 63.8 jit_solution(4339667921841356772)
XLA Ops:
  1.9 0.0 copy-start.1
  1.9 1.8 %pack.1 = f32[1600,128]{1,0:T(8,128)S(1)} custom-call(s32[1]{0:T(128)S(6)} %copy.16.bs_ref, s32[1]{0:T(128)S(6)} %copy.17.pe_ref, f32[8,16384]{1,0:T(8,128)} %st_hbm.1, f32[4,16384]{1,0:T(4,128)} %in_hbm.1), custom_call_target="tpu_custom_call" | custom-call | tf_op jit(solution)/shard_map/pack/pallas_call | solution.py:105
  3.8 0.0 copy-start
  3.8 0.0 copy-start.2
  3.8 39.1 %all_to_all.10 = f32[64,1,3200]{2,1,0:T(1,128)S(1)} all-to-all(f32[64,1,3200]{2,1,0:T(1,128)S(1)} %bitcast.6), channel_id=1, replica_groups=mesh['plant'=8,'section'=64] {'section'}, dimensions={0} | all-to-all | bytes 1638400 | tf_op jit(solution)/shard_map/all_to_all | solution.py:302
  42.8 0.0 copy-done.1
  42.8 0.0 copy-done
  42.8 0.0 copy-done.2
  42.8 4.9 %iterate.1 = (f32[512,256]{1,0:T(8,128)S(1)}, f32[256,256]{1,0:T(8,128)S(1)}, f32[512,256]{1,0:T(8,128)S(1)}, f32[64,128]{1,0:T(8,128)}) custom-call(s32[1]{0:T(128)S(6)} %copy.16.bs_ref, s32[1]{0:T(128)S(6)} %copy.17.pe_ref, f32[1600,128]{1,0:T(8,128)S(1)} %bitcast.5, bf16[512,512]{1,0:T(8,128)(2,1)S(1)} %copy-done.1, bf16[512,256]{1,0:T(8,128)(2,1)S(1)} %copy-done.2, ...), custom_call_target="tpu_custom_call" | custom-call | tf_op jit(solution)/shard_map/iterate/pallas_call | solution.py:276
  47.7 5.9 %all-to-all-start.1 = ((f32[64,1,128]{2,1,0:T(1,128)}), f32[64,1,128]{2,1,0:T(1,128)S(1)}, u32[]{:S(2)}, u32[]{:S(2)}) async-start(f32[64,1,128]{2,1,0:T(1,128)} %bitcast.3), calls=%async_computation.1 | async-start | bytes 65536 | tf_op jit(solution)/shard_map/all_to_all | solution.py:302
  53.6 0.8 %copy.13 = f32[512,256]{1,0:T(8,128)} copy(f32[512,256]{1,0:T(8,128)S(1)} %get-tuple-element.12) | data formatting | bytes 1048576
  54.4 0.7 %copy.14 = f32[256,256]{1,0:T(8,128)} copy(f32[256,256]{1,0:T(8,128)S(1)} %get-tuple-element.13) | data formatting | bytes 524288
  55.1 0.8 %copy.15 = f32[512,256]{1,0:T(8,128)} copy(f32[512,256]{1,0:T(8,128)S(1)} %get-tuple-element.14) | data formatting | bytes 1048576
  55.9 7.3 %all-to-all-done.1 = f32[64,1,128]{2,1,0:T(1,128)S(1)} async-done(((f32[64,1,128]{2,1,0:T(1,128)}), f32[64,1,128]{2,1,0:T(1,128)S(1)}, u32[]{:S(2)}, u32[]{:S(2)}) %all-to-all-start.1) | async-done | bytes 32800 | tf_op jit(solution)/shard_map/all_to_all | solution.py:302
  63.2 0.1 slice_reduce_fusion
  63.3 0.5 sqrt.3
Async XLA Ops:
  1.9 40.9 %copy-start.1 = (bf16[512,512]{1,0:T(8,128)(2,1)S(1)}, bf16[512,512]{1,0:T(8,128)(2,1)}, u32[]{:S(2)}) copy-start(bf16[512,512]{1,0:T(8,128)(2,1)} %a_ref.1) | copy-start | bytes 1572868
  3.8 39.1 %copy-start = (bf16[768,768]{1,0:T(8,128)(2,1)S(1)}, bf16[768,768]{1,0:T(8,128)(2,1)}, u32[]{:S(2)}) copy-start(bf16[768,768]{1,0:T(8,128)(2,1)} %k_ref.1) | copy-start | bytes 3538948
  3.8 39.1 %copy-start.2 = (bf16[512,256]{1,0:T(8,128)(2,1)S(1)}, bf16[512,256]{1,0:T(8,128)(2,1)}, u32[]{:S(2)}) copy-start(bf16[512,256]{1,0:T(8,128)(2,1)} %b_ref.1) | copy-start | bytes 786436
  47.7 15.5 %all-to-all-start.1 = ((f32[64,1,128]{2,1,0:T(1,128)}), f32[64,1,128]{2,1,0:T(1,128)S(1)}, u32[]{:S(2)}, u32[]{:S(2)}) async-start(f32[64,1,128]{2,1,0:T(1,128)} %bitcast.3), calls=%async_computation.1 | async-start | bytes 65536 | tf_op jit(solution)/shard_map/all_to_all | solution.py:302

commit v5 on v4

--- a/solution.py
+++ b/solution.py
@@ -280,7 +280,7 @@
             pltpu.VMEM((states, width), jnp.float32),
             pltpu.VMEM((controls, width), jnp.float32),
             pltpu.VMEM((states, width), jnp.float32),
-            pltpu.VMEM((parts, LANES), jnp.float32),
+            jax.ShapeDtypeStruct((parts, LANES), jnp.float32),
         ),
         in_specs=[smem, smem, vmem, vmem, vmem, vmem],
         out_specs=(vmem, vmem, vmem, vmem),
@@ -297,6 +297,32 @@
     )(block_start, period, received, dynamics, gain, inverse)
 
 
+def finish(sums, *blocks):
+    def body(sums_ref, *refs):
+        sources, sinks = refs[: len(blocks)], refs[len(blocks) : 2 * len(blocks)]
+        norms_ref, sems = refs[-2:]
+        copies = [pltpu.make_async_copy(a, b, sems.at[i]) for i, (a, b) in enumerate(zip(sources, sinks))]
+        for copy in copies:
+            copy.start()
+        norms_ref[...] = jnp.sqrt(jnp.sum(sums_ref[...], axis=0, keepdims=True))[:, :2]
+        for copy in copies:
+            copy.wait()
+
+    vmem = pl.BlockSpec(memory_space=pltpu.VMEM)
+    hbm = pl.BlockSpec(memory_space=pltpu.HBM)
+    return pl.pallas_call(
+        body,
+        name="finish",
+        out_shape=(
+            *[pltpu.HBM(b.shape, b.dtype) for b in blocks],
+            jax.ShapeDtypeStruct((1, 2), jnp.float32),
+        ),
+        in_specs=[vmem] * (1 + len(blocks)),
+        out_specs=(*[hbm] * len(blocks), vmem),
+        scratch_shapes=[pltpu.SemaphoreType.DMA((len(blocks),))],
+    )(*[pltpu.with_memory_space_constraint(b, pltpu.VMEM) for b in (sums, *blocks)])
+
+
 def swap(rows, parts):
     flat = rows.reshape(parts, 1, rows.size // parts)
     return lax.all_to_all(flat, "section", 0, 0, tiled=True)
@@ -307,8 +333,9 @@
     packed = pack(block_start, period, lin_state, lin_input, parts)
     received = swap(packed, parts).reshape(packed.shape)
     x, u, z, sums = iterate(block_start, period, received, dynamics, gain, inverse, parts)
-    sums = swap(sums, parts)
-    return x, u, z, jnp.sqrt(jnp.sum(sums[:, 0, :2], axis=0))
+    sums = swap(sums, parts).reshape(sums.shape)
+    x, u, z, norms = finish(sums, x, u, z)
+    return x, u, z, norms.reshape(2)
 
 
 def solution(mesh):

time: 64 us -> 64.2 us (level)
  blocking collectives: 39.1 us -> 54.3 us
  waiting for transfers between devices: 7.31 us -> 0 us
  starting transfers between devices: 5.86 us -> 0 us
  local copies, waits for them, and re-layouts: 2.83 us -> 0.02 us
  Pallas kernels: 6.69 us -> 7.71 us
    all_to_all x1 -> x2, blocking collectives: 39.1 us -> 54.3 us  [swap(): return lax.all_to_all(flat, 'section', 0, 0, tiled=True)]
    all_to_all x1 -> x0, waiting for transfers between devices: 7.31 us -> none  [swap(): return lax.all_to_all(flat, 'section', 0, 0, tiled=True)]
    all_to_all x1 -> x0, starting transfers between devices: 5.86 us -> none  [swap(): return lax.all_to_all(flat, 'section', 0, 0, tiled=True)]
    unnamed x9 -> x6, local copies, waits for them, and re-layouts: 2.31 us -> 0.02 us
    pallas_call x0 -> x1, Pallas kernels: none -> 1.59 us  [finish(): pl.pallas_call(body, name='finish', out_shape=(*[pltpu.HBM(b.shape, b.dty...]
  transfers between devices with their start and end apart: 1 -> 0, of which waited for: 1 -> 0; matrix products, arithmetic and copies ran while one was open for 4% -> 0% of each run, Pallas kernels for 0% -> 0%
where the time goes in v5:
time: 64.2 us; the launch traced here: 64 us
  blocking collectives  54.3 us (85%)
  Pallas kernels  7.71 us (12%)
  between operations  1.97 us (3%)
    all_to_all x2, blocking collectives, swap(): return lax.all_to_all(flat, 'section', 0, 0, tiled=True)  54.3 us
    pallas_call x1, Pallas kernels, iterate(): pl.pallas_call(body, name='iterate', out_shape=(pltpu.VMEM((states, width...  4.31 us
    pallas_call x1, Pallas kernels, pack(): pl.pallas_call(body, name='pack', out_shape=jax.ShapeDtypeStruct((parts *...  1.81 us
    pallas_call x1, Pallas kernels, finish(): pl.pallas_call(body, name='finish', out_shape=(*[pltpu.HBM(b.shape, b.dty...  1.59 us

profile of v5, /device:TPU:1, one launch (start us, length us, event | category | flops | bytes accessed | tf_op | source)
XLA Modules:
  0.0 64.0 jit_solution(18187454274645556002)
XLA Ops:
  1.9 0.0 copy-start.1
  1.9 1.8 %pack.1 = f32[1600,128]{1,0:T(8,128)S(1)} custom-call(s32[1]{0:T(128)S(6)} %copy.13.bs_ref, s32[1]{0:T(128)S(6)} %copy.14.pe_ref, f32[8,16384]{1,0:T(8,128)} %st_hbm.1, f32[4,16384]{1,0:T(4,128)} %in_hbm.1), custom_call_target="tpu_custom_call" | custom-call | tf_op jit(solution)/shard_map/pack/pallas_call | solution.py:105
  3.8 0.0 copy-start
  3.8 0.0 copy-start.2
  3.8 39.1 %all_to_all.10 = f32[64,1,3200]{2,1,0:T(1,128)S(1)} all-to-all(f32[64,1,3200]{2,1,0:T(1,128)S(1)} %bitcast.8), channel_id=1, replica_groups=mesh['plant'=8,'section'=64] {'section'}, dimensions={0} | all-to-all | bytes 1638400 | tf_op jit(solution)/shard_map/all_to_all | solution.py:328
  42.8 0.0 copy-done.1
  42.8 0.0 copy-done
  42.8 0.0 copy-done.2
  42.8 4.3 %iterate.1 = (f32[512,256]{1,0:T(8,128)S(1)}, f32[256,256]{1,0:T(8,128)S(1)}, f32[512,256]{1,0:T(8,128)S(1)}, f32[64,128]{1,0:T(8,128)S(1)}) custom-call(s32[1]{0:T(128)S(6)} %copy.13.bs_ref, s32[1]{0:T(128)S(6)} %copy.14.pe_ref, f32[1600,128]{1,0:T(8,128)S(1)} %bitcast.7, bf16[512,512]{1,0:T(8,128)(2,1)S(1)} %copy-done.1, bf16[512,256]{1,0:T(8,128)(2,1)S(1)} %copy-done.2, ...), custom_call_target="tpu_custom_call" | custom-call | tf_op jit(solution)/shard_map/iterate/pallas_call | solution.py:276
  47.2 15.3 %all_to_all.11 = f32[64,1,128]{2,1,0:T(1,128)S(1)} all-to-all(f32[64,1,128]{2,1,0:T(1,128)S(1)} %bitcast.10), channel_id=1, replica_groups=mesh['plant'=8,'section'=64] {'section'}, dimensions={0} | all-to-all | bytes 65536 | tf_op jit(solution)/shard_map/all_to_all | solution.py:328
  62.4 1.6 %finish.1 = (f32[512,256]{1,0:T(8,128)}, f32[256,256]{1,0:T(8,128)}, f32[512,256]{1,0:T(8,128)}, f32[1,2]{1,0:T(1,128)}) custom-call(f32[64,128]{1,0:T(8,128)S(1)} %bitcast.9, f32[512,256]{1,0:T(8,128)S(1)} %get-tuple-element.13.refs_0_, f32[256,256]{1,0:T(8,128)S(1)} %get-tuple-element.14.refs_1_, f32[512,256]{1,0:T(8,128)S(1)} %get-tuple-element.15.refs_2_), custom_call_target="tpu_custom_call" | custom-call | tf_op jit(solution)/shard_map/finish/pallas_call | solution.py:313
Async XLA Ops:
  1.9 40.9 %copy-start.1 = (bf16[512,512]{1,0:T(8,128)(2,1)S(1)}, bf16[512,512]{1,0:T(8,128)(2,1)}, u32[]{:S(2)}) copy-start(bf16[512,512]{1,0:T(8,128)(2,1)} %a_ref.1) | copy-start | bytes 1572868
  3.8 39.1 %copy-start = (bf16[768,768]{1,0:T(8,128)(2,1)S(1)}, bf16[768,768]{1,0:T(8,128)(2,1)}, u32[]{:S(2)}) copy-start(bf16[768,768]{1,0:T(8,128)(2,1)} %k_ref.1) | copy-start | bytes 3538948
  3.8 39.1 %copy-start.2 = (bf16[512,256]{1,0:T(8,128)(2,1)S(1)}, bf16[512,256]{1,0:T(8,128)(2,1)}, u32[]{:S(2)}) copy-start(bf16[512,256]{1,0:T(8,128)(2,1)} %b_ref.1) | copy-start | bytes 786436

commit v6 on v5

--- a/solution.py
+++ b/solution.py
@@ -300,11 +300,13 @@
 def finish(sums, *blocks):
     def body(sums_ref, *refs):
         sources, sinks = refs[: len(blocks)], refs[len(blocks) : 2 * len(blocks)]
-        norms_ref, sems = refs[-2:]
+        norms_hbm, norms_ref, sems = refs[-3:]
         copies = [pltpu.make_async_copy(a, b, sems.at[i]) for i, (a, b) in enumerate(zip(sources, sinks))]
         for copy in copies:
             copy.start()
         norms_ref[...] = jnp.sqrt(jnp.sum(sums_ref[...], axis=0, keepdims=True))[:, :2]
+        copies.append(pltpu.make_async_copy(norms_ref, norms_hbm, sems.at[len(blocks)]))
+        copies[-1].start()
         for copy in copies:
             copy.wait()
 
@@ -315,11 +317,11 @@
         name="finish",
         out_shape=(
             *[pltpu.HBM(b.shape, b.dtype) for b in blocks],
-            jax.ShapeDtypeStruct((1, 2), jnp.float32),
+            pltpu.HBM((1, 2), jnp.float32),
         ),
         in_specs=[vmem] * (1 + len(blocks)),
-        out_specs=(*[hbm] * len(blocks), vmem),
-        scratch_shapes=[pltpu.SemaphoreType.DMA((len(blocks),))],
+        out_specs=(*[hbm] * len(blocks), hbm),
+        scratch_shapes=[pltpu.VMEM((1, 2), jnp.float32), pltpu.SemaphoreType.DMA((len(blocks) + 1,))],
     )(*[pltpu.with_memory_space_constraint(b, pltpu.VMEM) for b in (sums, *blocks)])
 
 

time: 64.2 us -> 63.7 us (level)
  no operation moved by 1% of the time
where the time goes in v6:
time: 63.7 us; the launch traced here: 63.5 us
  blocking collectives  54.3 us (85%)
  Pallas kernels  7.21 us (11%)
  between operations  1.97 us (3%)
    all_to_all x2, blocking collectives, swap(): return lax.all_to_all(flat, 'section', 0, 0, tiled=True)  54.3 us
    pallas_call x1, Pallas kernels, iterate(): pl.pallas_call(body, name='iterate', out_shape=(pltpu.VMEM((states, width...  4.31 us
    pallas_call x1, Pallas kernels, pack(): pl.pallas_call(body, name='pack', out_shape=jax.ShapeDtypeStruct((parts *...  1.81 us

profile of v6, /device:TPU:1, one launch (start us, length us, event | category | flops | bytes accessed | tf_op | source)
XLA Modules:
  0.0 63.5 jit_solution(12435443181748920315)
XLA Ops:
  1.9 0.0 copy-start.1
  1.9 1.8 %pack.1 = f32[1600,128]{1,0:T(8,128)S(1)} custom-call(s32[1]{0:T(128)S(6)} %copy.13.bs_ref, s32[1]{0:T(128)S(6)} %copy.14.pe_ref, f32[8,16384]{1,0:T(8,128)} %st_hbm.1, f32[4,16384]{1,0:T(4,128)} %in_hbm.1), custom_call_target="tpu_custom_call" | custom-call | tf_op jit(solution)/shard_map/pack/pallas_call | solution.py:105
  3.8 0.0 copy-start
  3.8 0.0 copy-start.2
  3.8 39.1 %all_to_all.10 = f32[64,1,3200]{2,1,0:T(1,128)S(1)} all-to-all(f32[64,1,3200]{2,1,0:T(1,128)S(1)} %bitcast.8), channel_id=1, replica_groups=mesh['plant'=8,'section'=64] {'section'}, dimensions={0} | all-to-all | bytes 1638400 | tf_op jit(solution)/shard_map/all_to_all | solution.py:330
  42.8 0.0 copy-done.1
  42.8 0.0 copy-done
  42.8 0.0 copy-done.2
  42.8 4.3 %iterate.1 = (f32[512,256]{1,0:T(8,128)S(1)}, f32[256,256]{1,0:T(8,128)S(1)}, f32[512,256]{1,0:T(8,128)S(1)}, f32[64,128]{1,0:T(8,128)S(1)}) custom-call(s32[1]{0:T(128)S(6)} %copy.13.bs_ref, s32[1]{0:T(128)S(6)} %copy.14.pe_ref, f32[1600,128]{1,0:T(8,128)S(1)} %bitcast.7, bf16[512,512]{1,0:T(8,128)(2,1)S(1)} %copy-done.1, bf16[512,256]{1,0:T(8,128)(2,1)S(1)} %copy-done.2, ...), custom_call_target="tpu_custom_call" | custom-call | tf_op jit(solution)/shard_map/iterate/pallas_call | solution.py:276
  47.2 15.3 %all_to_all.11 = f32[64,1,128]{2,1,0:T(1,128)S(1)} all-to-all(f32[64,1,128]{2,1,0:T(1,128)S(1)} %bitcast.10), channel_id=1, replica_groups=mesh['plant'=8,'section'=64] {'section'}, dimensions={0} | all-to-all | bytes 65536 | tf_op jit(solution)/shard_map/all_to_all | solution.py:330
  62.4 1.1 %finish.1 = (f32[512,256]{1,0:T(8,128)}, f32[256,256]{1,0:T(8,128)}, f32[512,256]{1,0:T(8,128)}, f32[1,2]{1,0:T(1,128)}) custom-call(f32[64,128]{1,0:T(8,128)S(1)} %bitcast.9, f32[512,256]{1,0:T(8,128)S(1)} %get-tuple-element.13.refs_0_, f32[256,256]{1,0:T(8,128)S(1)} %get-tuple-element.14.refs_1_, f32[512,256]{1,0:T(8,128)S(1)} %get-tuple-element.15.refs_2_), custom_call_target="tpu_custom_call" | custom-call | tf_op jit(solution)/shard_map/finish/pallas_call | solution.py:315
Async XLA Ops:
  1.9 40.9 %copy-start.1 = (bf16[512,512]{1,0:T(8,128)(2,1)S(1)}, bf16[512,512]{1,0:T(8,128)(2,1)}, u32[]{:S(2)}) copy-start(bf16[512,512]{1,0:T(8,128)(2,1)} %a_ref.1) | copy-start | bytes 1572868
  3.8 39.1 %copy-start = (bf16[768,768]{1,0:T(8,128)(2,1)S(1)}, bf16[768,768]{1,0:T(8,128)(2,1)}, u32[]{:S(2)}) copy-start(bf16[768,768]{1,0:T(8,128)(2,1)} %k_ref.1) | copy-start | bytes 3538948
  3.8 39.1 %copy-start.2 = (bf16[512,256]{1,0:T(8,128)(2,1)S(1)}, bf16[512,256]{1,0:T(8,128)(2,1)}, u32[]{:S(2)}) copy-start(bf16[512,256]{1,0:T(8,128)(2,1)} %b_ref.1) | copy-start | bytes 786436

commit v7 on v6

--- a/solution.py
+++ b/solution.py
@@ -18,16 +18,13 @@
     per = 2 * rows_state + 2 * rows_input + 1
     assert width == 2 * LANES and rows_state == 8 and rows_input == 4
 
-    pieces = 2
+    pieces = 1
     piece = total // pieces
 
-    def body(bs_ref, pe_ref, st_hbm, in_hbm, out_ref, st_ref, in_ref, st_first, in_first, flat_ref, sems):
-        bs = bs_ref[0]
-        pe = pe_ref[0]
-        opening = pl.ds(pl.multiple_of(bs * width, LANES), LANES)
+    def body(bs_hbm, pe_hbm, st_hbm, in_hbm, out_ref, bs_ref, pe_ref, st_ref, in_ref, flat_ref, sems):
         copies = [
-            pltpu.make_async_copy(st_hbm.at[:, opening], st_first, sems.at[0]),
-            pltpu.make_async_copy(in_hbm.at[:, opening], in_first, sems.at[1]),
+            pltpu.make_async_copy(bs_hbm, bs_ref, sems.at[0]),
+            pltpu.make_async_copy(pe_hbm, pe_ref, sems.at[1]),
         ]
         for q in range(pieces):
             at = slice(piece * q, piece * q + piece)
@@ -44,13 +41,14 @@
 
         copies[0].wait()
         copies[1].wait()
-        first = jnp.concatenate([st_first[...], in_first[...], spare], axis=0)
+        bs = bs_ref[0, 0]
+        pe = pe_ref[0, 0]
+        for copy in copies[2:]:
+            copy.wait()
+        first = tile(bs * width)
         onward = pltpu.roll(first, lax.rem(pe, LANES), 1)
         edges = []
         for q in range(4):
-            if q * pieces % 4 == 0:
-                copies[2 + 2 * (q * pieces // 4)].wait()
-                copies[3 + 2 * (q * pieces // 4)].wait()
             collected = jnp.zeros((16, LANES), jnp.float32)
             for e in range(16):
                 d = 16 * q + e
@@ -99,30 +97,24 @@
             lane < 64, pltpu.roll(flat, 1, 0), pltpu.roll(flat, parts - 1, 0)
         )
 
-    smem = pl.BlockSpec(memory_space=pltpu.SMEM)
     vmem = pl.BlockSpec(memory_space=pltpu.VMEM)
     hbm = pl.BlockSpec(memory_space=pltpu.HBM)
     return pl.pallas_call(
         body,
         name="pack",
         out_shape=jax.ShapeDtypeStruct((parts * per, LANES), jnp.float32),
-        in_specs=[smem, smem, hbm, hbm],
+        in_specs=[hbm, hbm, hbm, hbm],
         out_specs=vmem,
         scratch_shapes=[
+            pltpu.SMEM((1, 1), jnp.int32),
+            pltpu.SMEM((1, 1), jnp.int32),
             pltpu.VMEM(state.shape, jnp.float32),
             pltpu.VMEM(inputs.shape, jnp.float32),
-            pltpu.VMEM((rows_state, LANES), jnp.float32),
-            pltpu.VMEM((rows_input, LANES), jnp.float32),
             pltpu.VMEM((LANES, LANES), jnp.float32),
             pltpu.SemaphoreType.DMA((2 + 2 * pieces,)),
         ],
         compiler_params=pltpu.CompilerParams(vmem_limit_bytes=32 << 20),
-    )(
-        block_start,
-        period,
-        pltpu.with_memory_space_constraint(state, pltpu.HBM),
-        pltpu.with_memory_space_constraint(inputs, pltpu.HBM),
-    )
+    )(block_start, period, *[pltpu.with_memory_space_constraint(v, pltpu.HBM) for v in (state, inputs)])
 
 
 def iterate(block_start, period, received, dynamics, gain, inverse, parts):
@@ -138,8 +130,14 @@
     nn = (((1,), (0,)), ((), ()))
     tn = (((0,), (0,)), ((), ()))
 
-    def body(bs_ref, pe_ref, got_ref, a_ref, b_ref, k_ref, x_ref, u_ref, z_ref, sums_ref,
-             nd_ref, ys_ref, vs_ref, gn_ref, ab_ref, *tiled):
+    def body(bs_hbm, pe_hbm, got_ref, a_ref, b_ref, k_ref, x_ref, u_ref, z_ref, sums_ref,
+             bs_ref, pe_ref, sems, nd_ref, ys_ref, vs_ref, gn_ref, ab_ref, *tiled):
+        scalars = [
+            pltpu.make_async_copy(bs_hbm, bs_ref, sems.at[0]),
+            pltpu.make_async_copy(pe_hbm, pe_ref, sems.at[1]),
+        ]
+        for copy in scalars:
+            copy.start()
         tiles = states // LANES
         neg_refs = tiled[: both // LANES]
         ws_refs = tiled[both // LANES : 2 * both // LANES]
@@ -229,8 +227,10 @@
             wb = w.astype(jnp.bfloat16)
             primal, dual = 0.0, 0.0
             if last:
-                idx = lax.rem(lax.axis_index("section") - bs_ref[0] + parts, parts)
-                count = pe_ref[0] - idx * width
+                for copy in scalars:
+                    copy.wait()
+                idx = lax.rem(lax.axis_index("section") - bs_ref[0, 0] + parts, parts)
+                count = pe_ref[0, 0] - idx * width
                 row = lax.broadcasted_iota(jnp.int32, (width, span), 0)
                 here = run * (row & 7) + (row >> 3) < count
                 keep = lax.broadcasted_iota(jnp.int32, (LANES, width), 1) < count
@@ -271,7 +271,7 @@
                 lane = lax.broadcasted_iota(jnp.int32, (parts, LANES), 1)
                 sums_ref[...] = jnp.where(lane == 0, jnp.sum(primal), jnp.where(lane == 1, jnp.sum(dual), 0.0))
 
-    smem = pl.BlockSpec(memory_space=pltpu.SMEM)
+    hbm = pl.BlockSpec(memory_space=pltpu.HBM)
     vmem = pl.BlockSpec(memory_space=pltpu.VMEM)
     return pl.pallas_call(
         body,
@@ -282,9 +282,12 @@
             pltpu.VMEM((states, width), jnp.float32),
             jax.ShapeDtypeStruct((parts, LANES), jnp.float32),
         ),
-        in_specs=[smem, smem, vmem, vmem, vmem, vmem],
+        in_specs=[hbm, hbm, vmem, vmem, vmem, vmem],
         out_specs=(vmem, vmem, vmem, vmem),
         scratch_shapes=[
+            pltpu.SMEM((1, 1), jnp.int32),
+            pltpu.SMEM((1, 1), jnp.int32),
+            pltpu.SemaphoreType.DMA((2,)),
             pltpu.VMEM((rows, states), jnp.float32),
             pltpu.VMEM((rows, states), jnp.float32),
             pltpu.VMEM((rows, states), jnp.float32),
@@ -294,7 +297,14 @@
             *[pltpu.VMEM((width, LANES), jnp.float32)] * ((both + states) // LANES),
         ],
         compiler_params=pltpu.CompilerParams(vmem_limit_bytes=48 << 20),
-    )(block_start, period, received, dynamics, gain, inverse)
+    )(
+        block_start,
+        period,
+        received,
+        dynamics,
+        gain,
+        inverse,
+    )
 
 
 def finish(sums, *blocks):
@@ -332,6 +342,7 @@
 
 def local(dynamics, gain, inverse, lin_state, lin_input, block_start, period):
     parts = lax.axis_size("section")
+    block_start, period = block_start[None], period[None]
     packed = pack(block_start, period, lin_state, lin_input, parts)
     received = swap(packed, parts).reshape(packed.shape)
     x, u, z, sums = iterate(block_start, period, received, dynamics, gain, inverse, parts)

time: 63.7 us -> 64.6 us (1.014)
  Pallas kernels: 7.21 us -> 8.05 us
    pallas_call x1, Pallas kernels: 4.31 us -> 5.13 us  [iterate(): pl.pallas_call(body, name='iterate', out_shape=(pltpu.VMEM((states, width...]
where the time goes in v7:
time: 64.6 us; the launch traced here: 64.4 us
  blocking collectives  54.3 us (84%)
  Pallas kernels  8.05 us (12%)
  between operations  1.97 us (3%)
    all_to_all x2, blocking collectives, swap(): return lax.all_to_all(flat, 'section', 0, 0, tiled=True)  54.3 us
    pallas_call x1, Pallas kernels, iterate(): pl.pallas_call(body, name='iterate', out_shape=(pltpu.VMEM((states, width...  5.13 us
    pallas_call x1, Pallas kernels, pack(): pl.pallas_call(body, name='pack', out_shape=jax.ShapeDtypeStruct((parts *...  1.84 us

profile of v7, /device:TPU:1, one launch (start us, length us, event | category | flops | bytes accessed | tf_op | source)
XLA Modules:
  0.0 64.4 jit_solution(12971423876544961906)
XLA Ops:
  1.9 0.0 copy-start.1
  1.9 1.8 %pack.1 = f32[1600,128]{1,0:T(8,128)S(1)} custom-call(s32[1,1]{1,0:T(1,128)} %bitcast.9.bs_hbm, s32[1,1]{1,0:T(1,128)} %bitcast.11.pe_hbm, f32[8,16384]{1,0:T(8,128)} %st_hbm.1, f32[4,16384]{1,0:T(4,128)} %in_hbm.1), custom_call_target="tpu_custom_call" | custom-call | tf_op jit(solution)/shard_map/pack/pallas_call | solution.py:102
  3.8 0.0 copy-start
  3.8 0.0 copy-start.2
  3.8 39.1 %all_to_all.10 = f32[64,1,3200]{2,1,0:T(1,128)S(1)} all-to-all(f32[64,1,3200]{2,1,0:T(1,128)S(1)} %bitcast.14), channel_id=1, replica_groups=mesh['plant'=8,'section'=64] {'section'}, dimensions={0} | all-to-all | bytes 1638400 | tf_op jit(solution)/shard_map/all_to_all | solution.py:340
  42.9 0.0 copy-done.1
  42.9 0.0 copy-done
  42.9 0.0 copy-done.2
  42.9 5.1 %iterate.1 = (f32[512,256]{1,0:T(8,128)S(1)}, f32[256,256]{1,0:T(8,128)S(1)}, f32[512,256]{1,0:T(8,128)S(1)}, f32[64,128]{1,0:T(8,128)S(1)}) custom-call(s32[1,1]{1,0:T(1,128)} %bitcast.10.bs_hbm, s32[1,1]{1,0:T(1,128)} %bitcast.12.pe_hbm, f32[1600,128]{1,0:T(8,128)S(1)} %bitcast.13, bf16[512,512]{1,0:T(8,128)(2,1)S(1)} %copy-done.1, ...), custom_call_target="tpu_custom_call" | custom-call | tf_op jit(solution)/shard_map/iterate/pallas_call | solution.py:276
  48.0 15.3 %all_to_all.11 = f32[64,1,128]{2,1,0:T(1,128)S(1)} all-to-all(f32[64,1,128]{2,1,0:T(1,128)S(1)} %bitcast.16), channel_id=1, replica_groups=mesh['plant'=8,'section'=64] {'section'}, dimensions={0} | all-to-all | bytes 65536 | tf_op jit(solution)/shard_map/all_to_all | solution.py:340
  63.3 1.1 %finish.1 = (f32[512,256]{1,0:T(8,128)}, f32[256,256]{1,0:T(8,128)}, f32[512,256]{1,0:T(8,128)}, f32[1,2]{1,0:T(1,128)}) custom-call(f32[64,128]{1,0:T(8,128)S(1)} %bitcast.15, f32[512,256]{1,0:T(8,128)S(1)} %get-tuple-element.13.refs_0_, f32[256,256]{1,0:T(8,128)S(1)} %get-tuple-element.14.refs_1_, f32[512,256]{1,0:T(8,128)S(1)} %get-tuple-element.15.refs_2_), custom_call_target="tpu_custom_call" | custom-call | tf_op jit(solution)/shard_map/finish/pallas_call | solution.py:325
Async XLA Ops:
  1.9 40.9 %copy-start.1 = (bf16[512,512]{1,0:T(8,128)(2,1)S(1)}, bf16[512,512]{1,0:T(8,128)(2,1)}, u32[]{:S(2)}) copy-start(bf16[512,512]{1,0:T(8,128)(2,1)} %a_ref.1) | copy-start | bytes 1572868
  3.8 39.1 %copy-start = (bf16[768,768]{1,0:T(8,128)(2,1)S(1)}, bf16[768,768]{1,0:T(8,128)(2,1)}, u32[]{:S(2)}) copy-start(bf16[768,768]{1,0:T(8,128)(2,1)} %k_ref.1) | copy-start | bytes 3538948
  3.8 39.1 %copy-start.2 = (bf16[512,256]{1,0:T(8,128)(2,1)S(1)}, bf16[512,256]{1,0:T(8,128)(2,1)}, u32[]{:S(2)}) copy-start(bf16[512,256]{1,0:T(8,128)(2,1)} %b_ref.1) | copy-start | bytes 786436

commit v8 on v6

--- a/solution.py
+++ b/solution.py
@@ -21,7 +21,7 @@
     pieces = 2
     piece = total // pieces
 
-    def body(bs_ref, pe_ref, st_hbm, in_hbm, out_ref, st_ref, in_ref, st_first, in_first, flat_ref, sems):
+    def body(bs_ref, pe_ref, st_hbm, in_hbm, out_ref, st_ref, in_ref, st_first, in_first, sems):
         bs = bs_ref[0]
         pe = pe_ref[0]
         opening = pl.ds(pl.multiple_of(bs * width, LANES), LANES)
@@ -84,15 +84,25 @@
             slot = lane & 7
             value = jnp.where((block == before) & (slot < HALO), tail, edges[q])
             values.append(jnp.where((block == bs) & (slot >= HALO), head, value))
-        flat_ref[:, 0:64] = jnp.concatenate(values, axis=0).T
-        parts_of = [jnp.zeros((16, LANES), jnp.float32)] * 4
-        lane16 = lane[:16]
-        for h in range(8):
-            picked = flat_ref[pl.ds(h, 16, stride=8), :]
-            for q in range(4):
-                shift = (16 * h - 16 * q) % LANES
-                moved = pltpu.roll(picked, shift, 1) if shift else picked
-                parts_of[q] = jnp.where((lane16 >> 4) == h, moved, parts_of[q])
+        slots = [jnp.where((lane & 7) == h, 1.0, 0.0).astype(jnp.bfloat16) for h in range(8)]
+        device = lax.broadcasted_iota(jnp.int32, (16, LANES), 0)
+        pick = jnp.where((lane >> 3) == device, 1.0, 0.0).astype(jnp.bfloat16)
+        pick = jnp.concatenate([pick, pick, pick], axis=1)
+        parts_of = []
+        for value in values:
+            high = value.astype(jnp.bfloat16)
+            rest = value - high.astype(jnp.float32)
+            middle = rest.astype(jnp.bfloat16)
+            low = (rest - middle.astype(jnp.float32)).astype(jnp.bfloat16)
+            spread = [jnp.concatenate([part * slot for slot in slots], axis=0) for part in (high, middle, low)]
+            parts_of.append(
+                lax.dot_general(
+                    pick,
+                    jnp.concatenate(spread, axis=1),
+                    (((1,), (1,)), ((), ())),
+                    preferred_element_type=jnp.float32,
+                )
+            )
         flat = jnp.concatenate(parts_of, axis=0)
         lane = lax.broadcasted_iota(jnp.int32, (parts, LANES), 1)
         out_ref[pl.ds(per - 1, parts, stride=per), :] = jnp.where(
@@ -113,7 +123,6 @@
             pltpu.VMEM(inputs.shape, jnp.float32),
             pltpu.VMEM((rows_state, LANES), jnp.float32),
             pltpu.VMEM((rows_input, LANES), jnp.float32),
-            pltpu.VMEM((LANES, LANES), jnp.float32),
             pltpu.SemaphoreType.DMA((2 + 2 * pieces,)),
         ],
         compiler_params=pltpu.CompilerParams(vmem_limit_bytes=32 << 20),

time: 63.7 us -> 63.7 us (level)
  no operation moved by 1% of the time
where the time goes in v8:
time: 63.7 us; the launch traced here: 63.5 us
  blocking collectives  54.3 us (85%)
  Pallas kernels  7.16 us (11%)
  between operations  1.97 us (3%)
    all_to_all x2, blocking collectives, swap(): return lax.all_to_all(flat, 'section', 0, 0, tiled=True)  54.3 us
    pallas_call x1, Pallas kernels, iterate(): pl.pallas_call(body, name='iterate', out_shape=(pltpu.VMEM((states, width...  4.31 us
    pallas_call x1, Pallas kernels, pack(): pl.pallas_call(body, name='pack', out_shape=jax.ShapeDtypeStruct((parts *...  1.76 us

profile of v8, /device:TPU:1, one launch (start us, length us, event | category | flops | bytes accessed | tf_op | source)
XLA Modules:
  0.0 63.5 jit_solution(5689547833268819361)
XLA Ops:
  1.9 0.0 copy-start.1
  1.9 1.8 %pack.1 = f32[1600,128]{1,0:T(8,128)S(1)} custom-call(s32[1]{0:T(128)S(6)} %copy.13.bs_ref, s32[1]{0:T(128)S(6)} %copy.14.pe_ref, f32[8,16384]{1,0:T(8,128)} %st_hbm.1, f32[4,16384]{1,0:T(4,128)} %in_hbm.1), custom_call_target="tpu_custom_call" | custom-call | tf_op jit(solution)/shard_map/pack/pallas_call | solution.py:115
  3.7 0.0 copy-start
  3.7 0.0 copy-start.2
  3.7 39.1 %all_to_all.10 = f32[64,1,3200]{2,1,0:T(1,128)S(1)} all-to-all(f32[64,1,3200]{2,1,0:T(1,128)S(1)} %bitcast.8), channel_id=1, replica_groups=mesh['plant'=8,'section'=64] {'section'}, dimensions={0} | all-to-all | bytes 1638400 | tf_op jit(solution)/shard_map/all_to_all | solution.py:339
  42.8 0.0 copy-done.1
  42.8 0.0 copy-done
  42.8 0.0 copy-done.2
  42.8 4.3 %iterate.1 = (f32[512,256]{1,0:T(8,128)S(1)}, f32[256,256]{1,0:T(8,128)S(1)}, f32[512,256]{1,0:T(8,128)S(1)}, f32[64,128]{1,0:T(8,128)S(1)}) custom-call(s32[1]{0:T(128)S(6)} %copy.13.bs_ref, s32[1]{0:T(128)S(6)} %copy.14.pe_ref, f32[1600,128]{1,0:T(8,128)S(1)} %bitcast.7, bf16[512,512]{1,0:T(8,128)(2,1)S(1)} %copy-done.1, bf16[512,256]{1,0:T(8,128)(2,1)S(1)} %copy-done.2, ...), custom_call_target="tpu_custom_call" | custom-call | tf_op jit(solution)/shard_map/iterate/pallas_call | solution.py:285
  47.1 15.3 %all_to_all.11 = f32[64,1,128]{2,1,0:T(1,128)S(1)} all-to-all(f32[64,1,128]{2,1,0:T(1,128)S(1)} %bitcast.10), channel_id=1, replica_groups=mesh['plant'=8,'section'=64] {'section'}, dimensions={0} | all-to-all | bytes 65536 | tf_op jit(solution)/shard_map/all_to_all | solution.py:339
  62.4 1.1 %finish.1 = (f32[512,256]{1,0:T(8,128)}, f32[256,256]{1,0:T(8,128)}, f32[512,256]{1,0:T(8,128)}, f32[1,2]{1,0:T(1,128)}) custom-call(f32[64,128]{1,0:T(8,128)S(1)} %bitcast.9, f32[512,256]{1,0:T(8,128)S(1)} %get-tuple-element.13.refs_0_, f32[256,256]{1,0:T(8,128)S(1)} %get-tuple-element.14.refs_1_, f32[512,256]{1,0:T(8,128)S(1)} %get-tuple-element.15.refs_2_), custom_call_target="tpu_custom_call" | custom-call | tf_op jit(solution)/shard_map/finish/pallas_call | solution.py:324
Async XLA Ops:
  1.9 40.9 %copy-start.1 = (bf16[512,512]{1,0:T(8,128)(2,1)S(1)}, bf16[512,512]{1,0:T(8,128)(2,1)}, u32[]{:S(2)}) copy-start(bf16[512,512]{1,0:T(8,128)(2,1)} %a_ref.1) | copy-start | bytes 1572868
  3.7 39.1 %copy-start = (bf16[768,768]{1,0:T(8,128)(2,1)S(1)}, bf16[768,768]{1,0:T(8,128)(2,1)}, u32[]{:S(2)}) copy-start(bf16[768,768]{1,0:T(8,128)(2,1)} %k_ref.1) | copy-start | bytes 3538948
  3.7 39.1 %copy-start.2 = (bf16[512,256]{1,0:T(8,128)(2,1)S(1)}, bf16[512,256]{1,0:T(8,128)(2,1)}, u32[]{:S(2)}) copy-start(bf16[512,256]{1,0:T(8,128)(2,1)} %b_ref.1) | copy-start | bytes 786436
